TPU v7x, 768 devices: a whole 4x8x12 slice. The times are simulated.
768 devices in a mesh: lat: 32 (over y, x), lon: 4 (over z_hi), lev: 6 (over z_lo, core).
Axes of the slice: x: 4, y: 8, z: 12 (z_hi: 4, z_lo: 3; z = z_hi * 3 + z_lo), core: 2. Of those that a mesh axis runs over, the one named last changes fastest.
Arguments:
- gradient: float32 [132, 1024, 1536], P('lev', 'lat', 'lon'), may hold values from -6 to 6
- vertical: float32 [132, 132], replicated, may hold values from -0.5 to 0.5
- variance: float32 [132, 1024, 1536], P('lev', 'lat', 'lon'), may hold values from 0.25 to 4
Outputs:
- increment: float32 [132, 1024, 1536], P('lev', 'lat', 'lon')
All inputs are finite; a program needn't handle non-finite values.
Results may differ from a plain program's by a relative error of at most 0.000078.
Values sent between devices are 32-bit elements; how exact they have to be, the bound alone decides.
No kernel may reach another device: no remote copies, remote signals or barrier semaphores. Data moves between devices by JAX's collectives and lax.ppermute only.
A program may use at most 32 MiB of HBM per device.

v0:
```python
import jax
import jax.numpy as jnp
from jax import lax
from jax.sharding import PartitionSpec as P

HALO = 32


def extended(cells, sides, width, closed):
    for axis, dim in sides:
        count = lax.axis_size(axis)
        ends = count if closed else count - 1
        head = lax.slice_in_dim(cells, 0, width, axis=dim)
        tail = lax.slice_in_dim(cells, cells.shape[dim] - width, cells.shape[dim], axis=dim)
        cells = jnp.concatenate(
            [
                lax.ppermute(tail, axis, [(i, (i + 1) % count) for i in range(ends)]),
                cells,
                lax.ppermute(head, axis, [((i + 1) % count, i) for i in range(ends)]),
            ],
            axis=dim,
        )
    return cells


def banded(count_out, count_in):
    outer = lax.broadcasted_iota(jnp.int32, (count_out, count_in), 0)
    inner = lax.broadcasted_iota(jnp.int32, (count_out, count_in), 1)
    offset = (inner - outer - HALO).astype(jnp.float32)
    taps = jnp.arange(-HALO, HALO + 1).astype(jnp.float32)
    bell = jnp.exp(-0.5 * (2.0 * taps / HALO) ** 2)
    scale = 1.0 / (jnp.sqrt(jnp.sum(bell)) * jnp.sqrt(jnp.sqrt(jnp.sum(bell * bell))))
    values = jnp.exp(-0.5 * (2.0 * offset / HALO) ** 2) * scale
    return jnp.where(jnp.abs(offset) <= HALO, values, 0.0)


def along_lat(field):
    padded = extended(field, (("lat", 1),), HALO, False)
    matrix = banded(field.shape[1], padded.shape[1])
    return jnp.einsum("ip,lpj->lij", matrix, padded, precision=lax.Precision.HIGHEST)


def along_lon(field):
    padded = extended(field, (("lon", 2),), HALO, True)
    matrix = banded(field.shape[2], padded.shape[2]).T
    return jnp.einsum("lip,pj->lij", padded, matrix, precision=lax.Precision.HIGHEST)


def on_device(gradient, vertical, variance):
    levels, rows, cols = gradient.shape
    own_rows = lax.dynamic_slice_in_dim(vertical, lax.axis_index("lev") * levels, levels, 0)
    start_total = jnp.zeros((levels, rows, cols), jnp.float32)
    piece = lax.all_gather(gradient, "lev", axis=0, tiled=True)
    mixed = jnp.dot(own_rows, piece.reshape(piece.shape[0], -1), precision=lax.Precision.HIGHEST)
    columns = mixed.reshape(start_total.shape)
    smooth = along_lon(along_lat(columns))
    scaled = variance * smooth
    return along_lat(along_lon(scaled))


def solution(mesh):
    return jax.shard_map(
        on_device,
        mesh=mesh,
        in_specs=(P("lev", "lat", "lon"), P(), P("lev", "lat", "lon")),
        out_specs=P("lev", "lat", "lon"),
        check_vma=False,
    )
```

profile of v0, /device:TPU:32, one launch (start us, length us, event | category | flops | bytes accessed | tf_op | source)
XLA Modules:
  0.0 256.3 jit_solution(2985410046644534337)
XLA Ops:
  6.5 0.0 copy-start
  6.5 0.0 all-gather.2.cloned.1.call-start
  6.5 0.7 all-gather.2.cloned.1.call-update
  7.3 88.4 %all-gather.2.cloned.1.call-done = f32[132,32,384]{2,1,0:T(8,128)} async-done(((f32[22,32,384]{2,1,0:T(8,128)}), f32[132,32,384]{2,1,0:T(8,128)}) %all-gather.2.cloned.1.call-update) | async-done | bytes 6488080 | tf_op jit(solution)/shard_map/all_gather | solution.py:53
  95.7 3.4 %slice_bitcast_fusion = f32[32,384,132]{1,0,2:T(8,128)S(1)} fusion(f32[132,32,384]{2,1,0:T(8,128)} %all-gather.2.cloned.1.call-done), kind=kLoop, calls=%fused_computation.2 | loop fusion | bytes 12976128 | tf_op jit(solution)/shard_map/dot_general | solution.py:54
  99.0 0.0 copy-done
  99.0 6.9 %fusion = f32[22,32,384]{2,0,1:T(8,128)S(1)} fusion(f32[32,384,132]{1,0,2:T(8,128)S(1)} %slice_bitcast_fusion, f32[132,132]{1,0:T(8,128)S(1)} %copy-done, s32[]{:T(128)S(6)} %select_n.13), kind=kOutput, calls=%fused_computation | convolution fusion | flops 428212224 | bytes 7593988 | tf_op jit(solution)/shard_map/dot_general | solution.py:54
  105.9 0.2 copy.8
  106.1 4.6 %collective-permute-start.1 = (f32[22,32,384]{2,1,0:T(8,128)S(1)}, f32[22,32,384]{2,1,0:T(8,128)}, u32[]{:S(2)}, u32[]{:S(2)}) collective-permute-start(f32[22,32,384]{2,1,0:T(8,128)S(1)} %copy.8), channel_id=1, source_target_pairs={{24,0},{48,24},{72,48},{96,72},{120,96},{144,120},{168,144},{192,1... | collective-permute-start | bytes 3244040 | tf_op jit(solution)/shard_map/ppermute | solution.py:19
  110.7 2.1 collective-permute-start
  112.8 0.6 fusion.61
  114.1 0.6 multiply_reduce_fusion
  115.5 19.3 %collective-permute-done.1 = f32[22,32,384]{2,1,0:T(8,128)} collective-permute-done((f32[22,32,384]{2,1,0:T(8,128)S(1)}, f32[22,32,384]{2,1,0:T(8,128)}, u32[]{:S(2)}, u32[]{:S(2)}) %collective-permute-start.1) | collective-permute-done | bytes 1081376 | tf_op jit(solution)/shard_map/ppermute | solution.py:19
  134.9 1.9 copy.11
  136.7 5.6 %collective-permute-done = f32[22,32,384]{2,1,0:T(8,128)S(1)} collective-permute-done((f32[22,32,384]{2,1,0:T(8,128)S(1)}, f32[22,32,384]{2,1,0:T(8,128)S(1)}, u32[]{:S(2)}, u32[]{:S(2)}) %collective-permute-start) | collective-permute-done | bytes 1081376 | tf_op jit(solution)/shard_map/ppermute | solution.py:17
  142.3 0.6 copy.10
  142.9 0.2 pad_maximum_fusion
  143.2 2.2 fusion.25
  145.4 0.0 copy-start.1
  145.4 0.2 fusion.87
  145.5 6.4 %collective-permute-start.3 = (f32[22,32,32]{2,1,0:T(8,128)S(1)}, f32[22,32,32]{2,1,0:T(8,128)S(1)}, u32[]{:S(2)}, u32[]{:S(2)}) collective-permute-start(f32[22,32,32]{2,1,0:T(8,128)S(1)} %get-tuple-element.8), channel_id=1, source_target_pairs={{6,0},{12,6},{18,12},{0,18},{7,1},{13,7},{19,13},{1,19},{8,2},{14,... | collective-permute-start | bytes 270344 | tf_op jit(solution)/shard_map/ppermute | solution.py:19
  151.9 2.6 %collective-permute-start.2 = (f32[22,32,32]{2,1,0:T(8,128)S(1)}, f32[22,32,32]{2,1,0:T(8,128)S(1)}, u32[]{:S(2)}, u32[]{:S(2)}) collective-permute-start(f32[22,32,32]{2,1,0:T(8,128)S(1)} %get-tuple-element.7), channel_id=1, source_target_pairs={{0,6},{6,12},{12,18},{18,0},{1,7},{7,13},{13,19},{19,1},{2,8},{8,1... | collective-permute-start | bytes 270344 | tf_op jit(solution)/shard_map/ppermute | solution.py:17
  154.5 20.7 %collective-permute-done.3 = f32[22,32,32]{2,1,0:T(8,128)S(1)} collective-permute-done((f32[22,32,32]{2,1,0:T(8,128)S(1)}, f32[22,32,32]{2,1,0:T(8,128)S(1)}, u32[]{:S(2)}, u32[]{:S(2)}) %collective-permute-start.3) | collective-permute-done | bytes 90144 | tf_op jit(solution)/shard_map/ppermute | solution.py:19
  175.2 7.1 %collective-permute-done.2 = f32[22,32,32]{2,1,0:T(8,128)S(1)} collective-permute-done((f32[22,32,32]{2,1,0:T(8,128)S(1)}, f32[22,32,32]{2,1,0:T(8,128)S(1)}, u32[]{:S(2)}, u32[]{:S(2)}) %collective-permute-start.2) | collective-permute-done | bytes 90144 | tf_op jit(solution)/shard_map/ppermute | solution.py:17
  182.3 0.0 copy-done.1
  182.3 2.8 %fusion.22 = f32[22,32,384]{2,1,0:T(8,128)S(1)} fusion(f32[22,32,384]{2,1,0:T(8,128)S(1)} %copy-done.1, f32[22,32,32]{2,1,0:T(8,128)S(1)} %collective-permute-done.3, f32[22,32,384]{2,1,0:T(8,128)S(1)} %fusion.25, f32[22,32,32]{2,1,0:T(8,128)S(1)} %collective-permute-done.2, f32[]{:T(128)S(6)} %div.32), kind=kOutput, calls=%fused_computation.24 | convolution fusion | flops 1455947776 | bytes 3424260 | tf_op jit(solution)/shard_map/lip,pj->lij/dot_general | solution.py:46
  185.1 0.2 fusion.86
  185.3 4.7 %collective-permute-start.5 = (f32[22,32,32]{2,1,0:T(8,128)S(1)}, f32[22,32,32]{2,1,0:T(8,128)S(1)}, u32[]{:S(2)}, u32[]{:S(2)}) collective-permute-start(f32[22,32,32]{2,1,0:T(8,128)S(1)} %get-tuple-element.6), channel_id=1, source_target_pairs={{6,0},{12,6},{18,12},{0,18},{7,1},{13,7},{19,13},{1,19},{8,2},{14,... | collective-permute-start | bytes 270344 | tf_op jit(solution)/shard_map/ppermute | solution.py:19
  189.9 3.0 %collective-permute-start.4 = (f32[22,32,32]{2,1,0:T(8,128)S(1)}, f32[22,32,32]{2,1,0:T(8,128)S(1)}, u32[]{:S(2)}, u32[]{:S(2)}) collective-permute-start(f32[22,32,32]{2,1,0:T(8,128)S(1)} %get-tuple-element.5), channel_id=1, source_target_pairs={{0,6},{6,12},{12,18},{18,0},{1,7},{7,13},{13,19},{19,1},{2,8},{8,1... | collective-permute-start | bytes 270344 | tf_op jit(solution)/shard_map/ppermute | solution.py:17
  192.9 16.4 %collective-permute-done.5 = f32[22,32,32]{2,1,0:T(8,128)S(1)} collective-permute-done((f32[22,32,32]{2,1,0:T(8,128)S(1)}, f32[22,32,32]{2,1,0:T(8,128)S(1)}, u32[]{:S(2)}, u32[]{:S(2)}) %collective-permute-start.5) | collective-permute-done | bytes 90144 | tf_op jit(solution)/shard_map/ppermute | solution.py:19
  209.3 1.7 collective-permute-done.4
  211.0 2.8 %fusion.16 = f32[22,32,384]{2,1,0:T(8,128)S(1)} fusion(f32[22,32,32]{2,1,0:T(8,128)S(1)} %collective-permute-done.5, f32[22,32,384]{2,1,0:T(8,128)S(1)} %fusion.22, f32[22,32,32]{2,1,0:T(8,128)S(1)} %collective-permute-done.4, f32[]{:T(128)S(6)} %div.32), kind=kOutput, calls=%fused_computation.18 | convolution fusion | flops 1455677440 | bytes 2342916 | tf_op jit(solution)/shard_map/lip,pj->lij/dot_general | solution.py:46
  213.8 1.9 collective-permute-start.7
  215.7 3.9 %collective-permute-start.6 = (f32[22,32,384]{2,1,0:T(8,128)S(1)}, f32[22,32,384]{2,1,0:T(8,128)S(1)}, u32[]{:S(2)}, u32[]{:S(2)}) collective-permute-start(f32[22,32,384]{2,1,0:T(8,128)S(1)} %fusion.16), channel_id=1, source_target_pairs={{0,24},{24,48},{48,72},{72,96},{96,120},{120,144},{144,168},{168,1... | collective-permute-start | bytes 3244040 | tf_op jit(solution)/shard_map/ppermute | solution.py:17
  219.7 21.6 %collective-permute-done.7 = f32[22,32,384]{2,1,0:T(8,128)S(1)} collective-permute-done((f32[22,32,384]{2,1,0:T(8,128)S(1)}, f32[22,32,384]{2,1,0:T(8,128)S(1)}, u32[]{:S(2)}, u32[]{:S(2)}) %collective-permute-start.7) | collective-permute-done | bytes 1081376 | tf_op jit(solution)/shard_map/ppermute | solution.py:19
  241.3 5.2 %collective-permute-done.6 = f32[22,32,384]{2,1,0:T(8,128)S(1)} collective-permute-done((f32[22,32,384]{2,1,0:T(8,128)S(1)}, f32[22,32,384]{2,1,0:T(8,128)S(1)}, u32[]{:S(2)}, u32[]{:S(2)}) %collective-permute-start.6) | collective-permute-done | bytes 1081376 | tf_op jit(solution)/shard_map/ppermute | solution.py:17
  246.6 2.9 %fusion.28 = f32[22,32,384]{2,1,0:T(8,128)} fusion(f32[22,32,384]{2,1,0:T(8,128)S(1)} %collective-permute-done.7, f32[22,32,384]{2,1,0:T(8,128)S(1)} %fusion.16, f32[22,32,384]{2,1,0:T(8,128)S(1)} %collective-permute-done.6, f32[]{:T(128)S(6)} %div.32), kind=kOutput, calls=%fused_computation.26 | convolution fusion | flops 313079808 | bytes 4325380 | tf_op jit(solution)/shard_map/ip,lpj->lij/dot_general | solution.py:40
Async XLA Ops:
  6.5 92.5 %copy-start = (f32[132,132]{1,0:T(8,128)S(1)}, f32[132,132]{1,0:T(8,128)}, u32[]{:S(2)}) copy-start(f32[132,132]{1,0:T(8,128)} %param.4) | copy-start | bytes 209092
  6.5 89.1 %all-gather.2.cloned.1.call-start = ((), (), s32[]{:S(2)}) async-start(), calls=%async_computation | async-start | bytes 7569408 | tf_op jit(solution)/shard_map/all_gather | solution.py:53
  106.1 28.7 %collective-permute-start.1 = (f32[22,32,384]{2,1,0:T(8,128)S(1)}, f32[22,32,384]{2,1,0:T(8,128)}, u32[]{:S(2)}, u32[]{:S(2)}) collective-permute-start(f32[22,32,384]{2,1,0:T(8,128)S(1)} %copy.8), channel_id=1, source_target_pairs={{24,0},{48,24},{72,48},{96,72},{120,96},{144,120},{168,144},{192,1... | collective-permute-start | bytes 3244040 | tf_op jit(solution)/shard_map/ppermute | solution.py:19
  110.7 31.6 %collective-permute-start = (f32[22,32,384]{2,1,0:T(8,128)S(1)}, f32[22,32,384]{2,1,0:T(8,128)S(1)}, u32[]{:S(2)}, u32[]{:S(2)}) collective-permute-start(f32[22,32,384]{2,1,0:T(8,128)S(1)} %copy.8), channel_id=1, source_target_pairs={{0,24},{24,48},{48,72},{72,96},{96,120},{120,144},{144,168},{168,1... | collective-permute-start | bytes 3244040 | tf_op jit(solution)/shard_map/ppermute | solution.py:17
  145.4 36.9 %copy-start.1 = (f32[22,32,384]{2,1,0:T(8,128)S(1)}, f32[22,32,384]{2,1,0:T(8,128)}, u32[]{:S(2)}) copy-start(f32[22,32,384]{2,1,0:T(8,128)} %param.5) | copy-start | bytes 3244036
  145.5 29.7 %collective-permute-start.3 = (f32[22,32,32]{2,1,0:T(8,128)S(1)}, f32[22,32,32]{2,1,0:T(8,128)S(1)}, u32[]{:S(2)}, u32[]{:S(2)}) collective-permute-start(f32[22,32,32]{2,1,0:T(8,128)S(1)} %get-tuple-element.8), channel_id=1, source_target_pairs={{6,0},{12,6},{18,12},{0,18},{7,1},{13,7},{19,13},{1,19},{8,2},{14,... | collective-permute-start | bytes 270344 | tf_op jit(solution)/shard_map/ppermute | solution.py:19
  151.9 30.3 %collective-permute-start.2 = (f32[22,32,32]{2,1,0:T(8,128)S(1)}, f32[22,32,32]{2,1,0:T(8,128)S(1)}, u32[]{:S(2)}, u32[]{:S(2)}) collective-permute-start(f32[22,32,32]{2,1,0:T(8,128)S(1)} %get-tuple-element.7), channel_id=1, source_target_pairs={{0,6},{6,12},{12,18},{18,0},{1,7},{7,13},{13,19},{19,1},{2,8},{8,1... | collective-permute-start | bytes 270344 | tf_op jit(solution)/shard_map/ppermute | solution.py:17
  185.3 24.0 %collective-permute-start.5 = (f32[22,32,32]{2,1,0:T(8,128)S(1)}, f32[22,32,32]{2,1,0:T(8,128)S(1)}, u32[]{:S(2)}, u32[]{:S(2)}) collective-permute-start(f32[22,32,32]{2,1,0:T(8,128)S(1)} %get-tuple-element.6), channel_id=1, source_target_pairs={{6,0},{12,6},{18,12},{0,18},{7,1},{13,7},{19,13},{1,19},{8,2},{14,... | collective-permute-start | bytes 270344 | tf_op jit(solution)/shard_map/ppermute | solution.py:19
  189.9 21.0 %collective-permute-start.4 = (f32[22,32,32]{2,1,0:T(8,128)S(1)}, f32[22,32,32]{2,1,0:T(8,128)S(1)}, u32[]{:S(2)}, u32[]{:S(2)}) collective-permute-start(f32[22,32,32]{2,1,0:T(8,128)S(1)} %get-tuple-element.5), channel_id=1, source_target_pairs={{0,6},{6,12},{12,18},{18,0},{1,7},{7,13},{13,19},{19,1},{2,8},{8,1... | collective-permute-start | bytes 270344 | tf_op jit(solution)/shard_map/ppermute | solution.py:17
  213.8 27.5 %collective-permute-start.7 = (f32[22,32,384]{2,1,0:T(8,128)S(1)}, f32[22,32,384]{2,1,0:T(8,128)S(1)}, u32[]{:S(2)}, u32[]{:S(2)}) collective-permute-start(f32[22,32,384]{2,1,0:T(8,128)S(1)} %fusion.16), channel_id=1, source_target_pairs={{24,0},{48,24},{72,48},{96,72},{120,96},{144,120},{168,144},{192,1... | collective-permute-start | bytes 3244040 | tf_op jit(solution)/shard_map/ppermute | solution.py:19
  215.7 30.8 %collective-permute-start.6 = (f32[22,32,384]{2,1,0:T(8,128)S(1)}, f32[22,32,384]{2,1,0:T(8,128)S(1)}, u32[]{:S(2)}, u32[]{:S(2)}) collective-permute-start(f32[22,32,384]{2,1,0:T(8,128)S(1)} %fusion.16), channel_id=1, source_target_pairs={{0,24},{24,48},{48,72},{72,96},{96,120},{120,144},{144,168},{168,1... | collective-permute-start | bytes 3244040 | tf_op jit(solution)/shard_map/ppermute | solution.py:17
Sparse Core Ops, SparseCore 0:
  9.7 85.8 all-gather.1
where the time goes:
time: 257 us; the launch traced here: 256 us
  waiting for transfers between devices  187 us (73%)
  starting transfers between devices  29.1 us (11%)
  matrix products  17.6 us (7%)
  between operations  15 us (6%)
  local copies, waits for them, and re-layouts  6.42 us (2%)
    all_gather x1, waiting for transfers between devices, on_device(): piece = lax.all_gather(gradient, 'lev', axis=0, tiled=True)  88.4 us
    ppermute x4, waiting for transfers between devices, extended(): lax.ppermute(head, axis, [((i + 1) % count, i) for i in range(ends)])  78 us
    ppermute x4, waiting for transfers between devices, extended(): lax.ppermute(tail, axis, [(i, (i + 1) % count) for i in range(ends)])  19.6 us
    ppermute x4, starting transfers between devices, extended(): lax.ppermute(head, axis, [((i + 1) % count, i) for i in range(ends)])  17.5 us
    ppermute x4, starting transfers between devices, extended(): lax.ppermute(tail, axis, [(i, (i + 1) % count) for i in range(ends)])  11.6 us
    dot_general x1, matrix products, on_device(): jnp.dot(own_rows, piece.reshape(piece.shape[0], -1), precision=lax.Precis...  6.87 us
    dot_general x2, matrix products, along_lon(): jnp.einsum('lip,pj->lij', padded, matrix, precision=lax.Precision.HIGHEST)  5.65 us
  transfers between devices with their start and end apart: 9, of which 9 were waited for; matrix products, arithmetic and copies ran while one was open for 1% of the time, Pallas kernels for 0%

commit v1 on v0

v1 whole, which is shorter than its diff:
```python
import math

import jax
import jax.numpy as jnp
from jax import lax
from jax.experimental import pallas as pl
from jax.experimental.pallas import tpu as pltpu
from jax.sharding import PartitionSpec as P


HALO = 32

LEVELS, ROWS, COLS = 22, 32, 384
DEVS = 6
PADDED = 24
TILE = 128
CUTS = 2
PART = LEVELS // CUTS


def tap_scale():
    taps = [math.exp(-0.5 * (2.0 * k / HALO) ** 2) for k in range(-HALO, HALO + 1)]
    return 1.0 / (math.sqrt(sum(taps)) * sum(t * t for t in taps) ** 0.25)


def weights(offset, valid):
    values = jnp.exp(-0.5 * (offset.astype(jnp.float32) * (2.0 / HALO)) ** 2) * tap_scale()
    return jnp.where(valid & (jnp.abs(offset) <= HALO), values, 0.0)


def split_outside(values):
    high = lax.reduce_precision(values, 8, 7)
    return high.astype(jnp.bfloat16), (values - high).astype(jnp.bfloat16)


def split(values):
    high = values.astype(jnp.bfloat16)
    return high, (values - high.astype(jnp.float32)).astype(jnp.bfloat16)


def iota(shape, dim):
    return lax.broadcasted_iota(jnp.int32, shape, dim)


def stored_column(k):
    tile, lane = k // TILE, k % TILE
    low = lane < 64
    edge = jnp.where(low, lane, 256 + lane)
    first = jnp.where(low, 128 + lane, lane)
    second = jnp.where(low, 256 + lane, 128 + lane)
    halo = jnp.where(low, 384 + lane, lane - 128)
    return jnp.where(tile == 0, edge, jnp.where(tile == 1, first, jnp.where(tile == 2, second, halo)))


def wide_column(n):
    m = n - COLS
    column = jnp.where(n < COLS, n, jnp.where(m < 64, n, m - TILE))
    return column, (n < COLS) | (m < HALO) | (m >= TILE - HALO)


def lon_matrices():
    wide = COLS + TILE
    shape = (wide, wide)
    out, valid = wide_column(iota(shape, 1))
    forward = weights(stored_column(iota(shape, 0)) - out, valid)
    shape = (wide, COLS)
    held, valid = wide_column(iota(shape, 0))
    adjoint = weights(held - iota(shape, 1), valid)
    return split_outside(forward) + split_outside(adjoint)


def lat_matrix():
    shape = (ROWS, 3 * ROWS)
    high, low = split_outside(weights(iota(shape, 1) - iota(shape, 0) - ROWS, jnp.full(shape, True)))
    return jnp.concatenate([high, low], axis=0)


def dot(a, b):
    return jnp.dot(a, b, preferred_element_type=jnp.float32)


def exact_right(left, right_high, right_low):
    high, low = split(left)
    return dot(high, right_high) + dot(low, right_high) + dot(high, right_low)


def exact_left(stacked, right):
    rows = stacked.shape[0] // 2
    high, low = split(right)
    both = dot(stacked, high)
    return both[:rows] + both[rows:] + dot(stacked[:rows], low)


def call(body, out_shape, **kwargs):
    return pl.pallas_call(body, out_shape=out_shape, compiler_params=pltpu.CompilerParams(vmem_limit_bytes=48 * 2**20), **kwargs)


def f32(*shape):
    return jax.ShapeDtypeStruct(shape, jnp.float32)


def pack_body(field, out):
    low = iota((LEVELS, 8, TILE), 2) < 64
    for band in range(4):
        t0, t1, t2 = (field[:, 8 * band : 8 * band + 8, TILE * k : TILE * k + TILE] for k in range(3))
        out[band] = jnp.where(low, t0, t2)
        out[4 + band] = jnp.where(low, t1, t0)
        out[8 + band] = jnp.where(low, t2, t1)


def mix_body(matrix, field, out, cells):
    high, low = split(matrix[...])
    cells[...] = jnp.zeros_like(cells)
    for piece in range(DEVS):
        for tile in range(2):
            for row in range(8):
                place = pl.ds((2 * piece + tile) * LEVELS * 8 + row, LEVELS, stride=8)
                cells[PADDED * piece : PADDED * piece + LEVELS, pl.ds((8 * tile + row) * TILE, TILE)] = field[place, :]
    for tile in range(2):
        cells_high, cells_low = split(cells[:, 8 * TILE * tile : 8 * TILE * (tile + 1)])
        mixed = dot(high, cells_high) + dot(low, cells_high) + dot(high, cells_low)
        for piece in range(DEVS):
            for row in range(8):
                place = pl.ds((2 * piece + tile) * LEVELS * 8 + row, LEVELS, stride=8)
                out[place, :] = mixed[PADDED * piece : PADDED * piece + LEVELS, TILE * row : TILE * row + TILE]


def edge_body(matrix, own, above, below, out, to_left, to_right):
    stacked = matrix[...]
    low = iota((16, TILE), 1) < 64
    for level in range(0, LEVELS, 2):
        pair = [
            jnp.concatenate([ref[band, lev] for ref in (above, own, below) for band in range(4)], axis=0)
            for lev in (level, level + 1)
        ]
        done = exact_left(stacked, jnp.concatenate(pair, axis=1))
        for k in range(2):
            edge = done[:, TILE * k : TILE * k + TILE]
            out[level + k] = edge
            top, bottom = edge[:16], pltpu.roll(edge[16:], 64, 1)
            to_left[level + k] = jnp.where(low, top, bottom)
            to_right[level + k] = jnp.where(low, bottom, top)


def inner_body(matrix, own, above, below, out):
    stacked = matrix[...]
    for level in range(LEVELS):
        sides = [
            jnp.concatenate([ref[4 * tile + band, level] for ref in (above, own, below) for band in range(4)], axis=0)
            for tile in range(2)
        ]
        out[level] = exact_left(stacked, jnp.concatenate(sides, axis=1))


def edges_body(field, to_left, to_right):
    group = iota((LEVELS, 8, TILE), 2) // HALO
    left, right = field[:, 0:8, 0:TILE], field[:, 24:32, 2 * TILE :]
    right = pltpu.roll(right, 96, 2)
    for band in range(1, 4):
        left = jnp.where(group == band, pltpu.roll(field[:, 8 * band : 8 * band + 8, 0:TILE], HALO * band, 2), left)
    for band in range(3):
        moved = field[:, 8 * band : 8 * band + 8, 2 * TILE :]
        if band:
            moved = pltpu.roll(moved, HALO * band, 2)
        right = jnp.where(group == (band + 3) % 4, moved, right)
    to_left[...] = left
    to_right[...] = right


def lon_body(edge, inner, from_left, from_right, variance, var_left, var_right, fwd_high, fwd_low, adj_high, adj_low, out):
    flat = (PART * ROWS, TILE)
    low = iota((PART, 16, TILE), 2) < 64
    left, right = from_left[...], from_right[...]
    top = jnp.where(low, right, left)
    bottom = pltpu.roll(jnp.where(low, left, right), 64, 2)
    halo = jnp.concatenate([top, bottom], axis=1).reshape(flat)
    held = jnp.concatenate([edge[...].reshape(flat), inner[...].reshape(PART * ROWS, 2 * TILE), halo], axis=1)
    smooth = exact_right(held, fwd_high[...], fwd_low[...])
    lane = iota((PART, 8, TILE), 2)
    left, right = var_left[...], var_right[...]
    bands = []
    for band in range(4):
        l, r = left, right
        if band:
            l, r = pltpu.roll(left, TILE - HALO * band, 2), pltpu.roll(right, TILE - HALO * band, 2)
        bands.append(jnp.where(lane < HALO, r, jnp.where(lane >= TILE - HALO, l, 0.0)))
    side = jnp.concatenate(bands, axis=1).reshape(flat)
    scale = jnp.concatenate([variance[...].reshape(PART * ROWS, COLS), side], axis=1)
    out[...] = exact_right(smooth * scale, adj_high[...], adj_low[...]).reshape(PART, ROWS, COLS)


def last_body(matrix, *refs):
    stacked = matrix[...]
    out = refs[-1]
    for part in range(CUTS):
        own, above, below = refs[3 * part : 3 * part + 3]
        for level in range(PART):
            cells = jnp.concatenate([above[level], own[level], below[level]], axis=0)
            out[part * PART + level] = exact_left(stacked, cells)


def shifted(cells, axis, step, closed):
    count = lax.axis_size(axis)
    pairs = [(i, (i + step) % count) for i in range(count) if closed or 0 <= i + step < count]
    return lax.ppermute(cells, axis, pairs)


def steps(gradient, vertical, variance):
    lat = lat_matrix()
    lon = lon_matrices()
    tiles = (2 * DEVS, LEVELS, 8, TILE)
    flat = (2 * DEVS * LEVELS * 8, TILE)
    matrix = jnp.pad(vertical.reshape(DEVS, LEVELS, DEVS, LEVELS), ((0, 0), (0, PADDED - LEVELS)) * 2).reshape(DEVS * PADDED, DEVS * PADDED)
    packed = call(pack_body, f32(*tiles))(gradient)
    gathered = lax.all_to_all(packed, "lev", 0, 0, tiled=True)
    scratch = [pltpu.VMEM((DEVS * PADDED, 16 * TILE), jnp.float32)]
    mixed = call(mix_body, f32(*flat), scratch_shapes=scratch)(matrix, gathered.reshape(flat)).reshape(tiles)
    mixed = lax.all_to_all(mixed, "lev", 0, 0, tiled=True)

    edge, inner = mixed[:4], mixed[4:]
    above, below = shifted(edge, "lat", 1, False), shifted(edge, "lat", -1, False)
    inner_above, inner_below = shifted(inner, "lat", 1, False), shifted(inner, "lat", -1, False)

    packed = f32(LEVELS, 16, TILE)
    edge, to_left, to_right = call(edge_body, (f32(LEVELS, ROWS, TILE), packed, packed))(lat, edge, above, below)
    from_left, from_right = shifted(to_right, "lon", 1, True), shifted(to_left, "lon", -1, True)
    var_side = f32(LEVELS, 8, TILE)
    to_left, to_right = call(edges_body, (var_side, var_side))(variance)
    var_left, var_right = shifted(to_right, "lon", 1, True), shifted(to_left, "lon", -1, True)
    inner = call(inner_body, f32(LEVELS, ROWS, 2 * TILE))(lat, inner, inner_above, inner_below)

    operands = []
    for cut in range(CUTS):
        def block(array, cut=cut):
            return pl.BlockSpec((PART,) + array.shape[1:], lambda i: (cut, 0, 0))

        arrays = (edge, inner, from_left, from_right, variance, var_left, var_right)
        specs = [block(a) for a in arrays] + [pl.BlockSpec(m.shape, lambda i: (0, 0)) for m in lon]
        spread = call(
            lon_body, f32(PART, ROWS, COLS), grid=(1,), in_specs=specs,
            out_specs=pl.BlockSpec((PART, ROWS, COLS), lambda i: (0, 0, 0)),
        )(*arrays, *lon)
        operands += [spread, shifted(spread, "lat", 1, False), shifted(spread, "lat", -1, False)]
    return call(last_body, f32(LEVELS, ROWS, COLS))(lat, *operands)


def solution(mesh):
    return jax.shard_map(
        steps,
        mesh=mesh,
        in_specs=(P("lev", "lat", "lon"), P(), P("lev", "lat", "lon")),
        out_specs=P("lev", "lat", "lon"),
        check_vma=False,
    )
```

time: 257 us -> 154 us (0.60)
  the two profiles are of different devices: /device:TPU:32 before, /device:TPU:96 now
where the time goes in v1:
time: 154 us
  starting transfers between devices  75.5 us (49%)
  waiting for transfers between devices  65.8 us (43%)
  Pallas kernels  8.47 us (6%)
  other arithmetic  2.19 us (1%)
  local copies, waits for them, and re-layouts  1.7 us (1%)
    ppermute x12, starting transfers between devices, shifted(): return lax.ppermute(cells, axis, pairs)  64.1 us
    ppermute x12, waiting for transfers between devices, shifted(): return lax.ppermute(cells, axis, pairs)  41.7 us
    all_to_all x1, waiting for transfers between devices, steps(): gathered = lax.all_to_all(packed, 'lev', 0, 0, tiled=True)  16.7 us
    all_to_all x1, waiting for transfers between devices, steps(): mixed = lax.all_to_all(mixed, 'lev', 0, 0, tiled=True)  7.41 us
    all_to_all x1, starting transfers between devices, steps(): mixed = lax.all_to_all(mixed, 'lev', 0, 0, tiled=True)  6.13 us
    all_to_all x1, starting transfers between devices, steps(): gathered = lax.all_to_all(packed, 'lev', 0, 0, tiled=True)  5.23 us
  transfers between devices with their start and end apart: 14, of which 9 were waited for; matrix products, arithmetic and copies ran while one was open for 2% of the time, Pallas kernels for 2%

profile of v1, /device:TPU:96, one launch (start us, length us, event | category | flops | bytes accessed | tf_op | source)
XLA Modules:
  0.0 153.9 jit_solution(9078659733952429453)
XLA Ops:
  0.0 0.0 copy-start.1
  0.0 1.2 copy-done.1
  1.2 1.1 shard_map.37
  2.3 0.0 copy-start.2
  2.3 5.2 %all-to-all-start = ((f32[12,22,8,128]{3,2,1,0:T(8,128)}), f32[12,22,8,128]{3,2,1,0:T(8,128)S(1)}, u32[]{:S(2)}, u32[]{:S(2)}) async-start(f32[12,22,8,128]{3,2,1,0:T(8,128)} %shard_map.37), calls=%async_computation | async-start | bytes 2162688 | tf_op jit(solution)/shard_map/all_to_all | solution.py:215
  7.5 0.0 copy-done.2
  7.5 0.2 reshape.12
  7.8 0.2 reshape.13.matrix
  7.9 16.7 %all-to-all-done = f32[12,22,8,128]{3,2,1,0:T(8,128)S(1)} async-done(((f32[12,22,8,128]{3,2,1,0:T(8,128)}), f32[12,22,8,128]{3,2,1,0:T(8,128)S(1)}, u32[]{:S(2)}, u32[]{:S(2)}) %all-to-all-start) | async-done | bytes 1081376 | tf_op jit(solution)/shard_map/all_to_all | solution.py:215
  24.6 1.8 %shard_map.38 = f32[2112,128]{1,0:T(8,128)} custom-call(f32[144,144]{1,0:T(8,128)S(1)} %reshape.13.matrix, f32[2112,128]{1,0:T(8,128)S(1)} %bitcast.2), custom_call_target="tpu_custom_call" | custom-call | tf_op jit(solution)/shard_map/pallas_call | solution.py:217
  26.4 0.0 copy-start
  26.4 6.1 %all-to-all-start.1 = ((f32[12,22,8,128]{3,2,1,0:T(8,128)}), f32[12,22,8,128]{3,2,1,0:T(8,128)S(1)}, u32[]{:S(2)}, u32[]{:S(2)}) async-start(f32[12,22,8,128]{3,2,1,0:T(8,128)} %bitcast.1), calls=%async_computation.1 | async-start | bytes 2162688 | tf_op jit(solution)/shard_map/all_to_all | solution.py:218
  32.6 0.0 copy-done
  32.6 0.2 shard_map.41
  32.8 11.5 %collective-permute-start.6 = (f32[22,8,128]{2,1,0:T(8,128)S(1)}, f32[22,8,128]{2,1,0:T(8,128)S(1)}, u32[]{:S(2)}, u32[]{:S(2)}) collective-permute-start(f32[22,8,128]{2,1,0:T(8,128)S(1)} %get-tuple-element.13), channel_id=1, source_target_pairs={{0,6},{6,12},{12,18},{18,0},{1,7},{7,13},{13,19},{19,1},{2,8},{8,1... | collective-permute-start | bytes 270344 | tf_op jit(solution)/shard_map/ppermute | solution.py:205
  44.4 7.4 %all-to-all-done.1 = f32[12,22,8,128]{3,2,1,0:T(8,128)S(1)} async-done(((f32[12,22,8,128]{3,2,1,0:T(8,128)}), f32[12,22,8,128]{3,2,1,0:T(8,128)S(1)}, u32[]{:S(2)}, u32[]{:S(2)}) %all-to-all-start.1) | async-done | bytes 1081376 | tf_op jit(solution)/shard_map/all_to_all | solution.py:218
  51.8 4.6 %collective-permute-start.3 = (f32[8,22,8,128]{3,2,1,0:T(8,128)S(1)}, f32[8,22,8,128]{3,2,1,0:T(8,128)S(1)}, u32[]{:S(2)}, u32[]{:S(2)}) collective-permute-start(f32[8,22,8,128]{3,2,1,0:T(8,128)S(1)} %slice.9.own), channel_id=1, source_target_pairs={{24,0},{48,24},{72,48},{96,72},{120,96},{144,120},{168,144},{192,1... | collective-permute-start | bytes 2162696 | tf_op jit(solution)/shard_map/ppermute | solution.py:205
  56.4 1.9 %collective-permute-start.2 = (f32[8,22,8,128]{3,2,1,0:T(8,128)S(1)}, f32[8,22,8,128]{3,2,1,0:T(8,128)S(1)}, u32[]{:S(2)}, u32[]{:S(2)}) collective-permute-start(f32[8,22,8,128]{3,2,1,0:T(8,128)S(1)} %slice.9.own), channel_id=1, source_target_pairs={{0,24},{24,48},{48,72},{72,96},{96,120},{120,144},{144,168},{168,1... | collective-permute-start | bytes 2162696 | tf_op jit(solution)/shard_map/ppermute | solution.py:205
  58.4 7.2 %collective-permute-start.1 = (f32[4,22,8,128]{3,2,1,0:T(8,128)S(1)}, f32[4,22,8,128]{3,2,1,0:T(8,128)S(1)}, u32[]{:S(2)}, u32[]{:S(2)}) collective-permute-start(f32[4,22,8,128]{3,2,1,0:T(8,128)S(1)} %slice.8.own), channel_id=1, source_target_pairs={{24,0},{48,24},{72,48},{96,72},{120,96},{144,120},{168,144},{192,1... | collective-permute-start | bytes 1081352 | tf_op jit(solution)/shard_map/ppermute | solution.py:205
  65.7 1.9 %collective-permute-start = (f32[4,22,8,128]{3,2,1,0:T(8,128)S(1)}, f32[4,22,8,128]{3,2,1,0:T(8,128)S(1)}, u32[]{:S(2)}, u32[]{:S(2)}) collective-permute-start(f32[4,22,8,128]{3,2,1,0:T(8,128)S(1)} %slice.8.own), channel_id=1, source_target_pairs={{0,24},{24,48},{48,72},{72,96},{96,120},{120,144},{144,168},{168,1... | collective-permute-start | bytes 1081352 | tf_op jit(solution)/shard_map/ppermute | solution.py:205
  67.6 1.1 fusion.6
  68.7 10.6 %collective-permute-done.1.below = f32[4,22,8,128]{3,2,1,0:T(8,128)S(1)} collective-permute-done((f32[4,22,8,128]{3,2,1,0:T(8,128)S(1)}, f32[4,22,8,128]{3,2,1,0:T(8,128)S(1)}, u32[]{:S(2)}, u32[]{:S(2)}) %collective-permute-start.1) | collective-permute-done | bytes 360480 | tf_op jit(solution)/shard_map/ppermute | solution.py:205
  79.4 12.8 %collective-permute-start.7 = (f32[22,8,128]{2,1,0:T(8,128)S(1)}, f32[22,8,128]{2,1,0:T(8,128)S(1)}, u32[]{:S(2)}, u32[]{:S(2)}) collective-permute-start(f32[22,8,128]{2,1,0:T(8,128)S(1)} %get-tuple-element.14), channel_id=1, source_target_pairs={{0,18},{6,0},{12,6},{18,12},{1,19},{7,1},{13,7},{19,13},{2,20},{8,... | collective-permute-start | bytes 270344 | tf_op jit(solution)/shard_map/ppermute | solution.py:205
  92.1 0.0 collective-permute-done.above
  92.2 0.4 shard_map.39
  92.6 8.1 %collective-permute-start.4 = (f32[22,16,128]{2,1,0:T(8,128)S(1)}, f32[22,16,128]{2,1,0:T(8,128)S(1)}, u32[]{:S(2)}, u32[]{:S(2)}) collective-permute-start(f32[22,16,128]{2,1,0:T(8,128)S(1)} %get-tuple-element.11), channel_id=1, source_target_pairs={{0,6},{6,12},{12,18},{18,0},{1,7},{7,13},{13,19},{19,1},{2,8},{8,1... | collective-permute-start | bytes 540680 | tf_op jit(solution)/shard_map/ppermute | solution.py:205
  100.7 0.0 collective-permute-done.3.below
  100.7 1.9 %collective-permute-start.5 = (f32[22,16,128]{2,1,0:T(8,128)S(1)}, f32[22,16,128]{2,1,0:T(8,128)S(1)}, u32[]{:S(2)}, u32[]{:S(2)}) collective-permute-start(f32[22,16,128]{2,1,0:T(8,128)S(1)} %get-tuple-element.12), channel_id=1, source_target_pairs={{0,18},{6,0},{12,6},{18,12},{1,19},{7,1},{13,7},{19,13},{2,20},{8,... | collective-permute-start | bytes 540680 | tf_op jit(solution)/shard_map/ppermute | solution.py:205
  102.6 1.0 fusion.8
  103.6 0.0 collective-permute-done.2.above
  103.6 0.5 shard_map.40.inner
  104.2 0.0 collective-permute-done.6.var_left
  104.2 0.0 collective-permute-done.7.var_right
  104.2 3.3 %collective-permute-done.4.from_left = f32[22,16,128]{2,1,0:T(8,128)S(1)} collective-permute-done((f32[22,16,128]{2,1,0:T(8,128)S(1)}, f32[22,16,128]{2,1,0:T(8,128)S(1)}, u32[]{:S(2)}, u32[]{:S(2)}) %collective-permute-start.4) | collective-permute-done | bytes 180256 | tf_op jit(solution)/shard_map/ppermute | solution.py:205
  107.5 10.0 %collective-permute-done.5.from_right = f32[22,16,128]{2,1,0:T(8,128)S(1)} collective-permute-done((f32[22,16,128]{2,1,0:T(8,128)S(1)}, f32[22,16,128]{2,1,0:T(8,128)S(1)}, u32[]{:S(2)}, u32[]{:S(2)}) %collective-permute-start.5) | collective-permute-done | bytes 180256 | tf_op jit(solution)/shard_map/ppermute | solution.py:205
  117.5 1.3 shard_map.42.refs_0_
  118.8 3.1 %collective-permute-start.9 = (f32[11,32,384]{2,1,0:T(8,128)S(1)}, f32[11,32,384]{2,1,0:T(8,128)S(1)}, u32[]{:S(2)}, u32[]{:S(2)}) collective-permute-start(f32[11,32,384]{2,1,0:T(8,128)S(1)} %shard_map.42.refs_0_), channel_id=1, source_target_pairs={{24,0},{48,24},{72,48},{96,72},{120,96},{144,120},{168,144},{192,1... | collective-permute-start | bytes 1622024 | tf_op jit(solution)/shard_map/ppermute | solution.py:205
  121.9 2.8 %collective-permute-start.8 = (f32[11,32,384]{2,1,0:T(8,128)S(1)}, f32[11,32,384]{2,1,0:T(8,128)S(1)}, u32[]{:S(2)}, u32[]{:S(2)}) collective-permute-start(f32[11,32,384]{2,1,0:T(8,128)S(1)} %shard_map.42.refs_0_), channel_id=1, source_target_pairs={{0,24},{24,48},{48,72},{72,96},{96,120},{120,144},{144,168},{168,1... | collective-permute-start | bytes 1622024 | tf_op jit(solution)/shard_map/ppermute | solution.py:205
  124.7 1.3 shard_map.43.refs_3_
  126.0 6.4 %collective-permute-start.11 = (f32[11,32,384]{2,1,0:T(8,128)S(1)}, f32[11,32,384]{2,1,0:T(8,128)S(1)}, u32[]{:S(2)}, u32[]{:S(2)}) collective-permute-start(f32[11,32,384]{2,1,0:T(8,128)S(1)} %shard_map.43.refs_3_), channel_id=1, source_target_pairs={{24,0},{48,24},{72,48},{96,72},{120,96},{144,120},{168,144},{192,1... | collective-permute-start | bytes 1622024 | tf_op jit(solution)/shard_map/ppermute | solution.py:205
  132.4 1.9 %collective-permute-start.10 = (f32[11,32,384]{2,1,0:T(8,128)S(1)}, f32[11,32,384]{2,1,0:T(8,128)S(1)}, u32[]{:S(2)}, u32[]{:S(2)}) collective-permute-start(f32[11,32,384]{2,1,0:T(8,128)S(1)} %shard_map.43.refs_3_), channel_id=1, source_target_pairs={{0,24},{24,48},{48,72},{72,96},{96,120},{120,144},{144,168},{168,1... | collective-permute-start | bytes 1622024 | tf_op jit(solution)/shard_map/ppermute | solution.py:205
  134.4 1.5 collective-permute-done.9.refs_2_
  135.9 6.2 %collective-permute-done.8.refs_1_ = f32[11,32,384]{2,1,0:T(8,128)S(1)} collective-permute-done((f32[11,32,384]{2,1,0:T(8,128)S(1)}, f32[11,32,384]{2,1,0:T(8,128)S(1)}, u32[]{:S(2)}, u32[]{:S(2)}) %collective-permute-start.8) | collective-permute-done | bytes 540704 | tf_op jit(solution)/shard_map/ppermute | solution.py:205
  142.1 4.4 %collective-permute-done.11.refs_5_ = f32[11,32,384]{2,1,0:T(8,128)S(1)} collective-permute-done((f32[11,32,384]{2,1,0:T(8,128)S(1)}, f32[11,32,384]{2,1,0:T(8,128)S(1)}, u32[]{:S(2)}, u32[]{:S(2)}) %collective-permute-start.11) | collective-permute-done | bytes 540704 | tf_op jit(solution)/shard_map/ppermute | solution.py:205
  146.5 5.6 %collective-permute-done.10.refs_4_ = f32[11,32,384]{2,1,0:T(8,128)S(1)} collective-permute-done((f32[11,32,384]{2,1,0:T(8,128)S(1)}, f32[11,32,384]{2,1,0:T(8,128)S(1)}, u32[]{:S(2)}, u32[]{:S(2)}) %collective-permute-start.10) | collective-permute-done | bytes 540704 | tf_op jit(solution)/shard_map/ppermute | solution.py:205
  152.1 1.8 %shard_map.44 = f32[22,32,384]{2,1,0:T(8,128)} custom-call(bf16[64,96]{1,0:T(8,128)(2,1)S(1)} %pad_maximum_fusion.matrix, f32[11,32,384]{2,1,0:T(8,128)S(1)} %shard_map.42.refs_0_, f32[11,32,384]{2,1,0:T(8,128)S(1)} %collective-permute-done.8.refs_1_, f32[11,32,384]{2,1,0:T(8,128)S(1)} %collective-permute-done.9.refs_2_, ...), custom_call_target="tpu_custom_call" | custom-call | tf_op jit(solution)/shard_map/pallas_call | solution.py:244
  (11 shorter events, 0.2 us)
Async XLA Ops:
  0.0 1.2 copy-start.1
  2.3 5.2 %copy-start.2 = (f32[132,132]{1,0:T(8,128)S(1)}, f32[132,132]{1,0:T(8,128)}, u32[]{:S(2)}) copy-start(f32[132,132]{1,0:T(8,128)} %param.4) | copy-start | bytes 209092
  2.3 22.3 %all-to-all-start = ((f32[12,22,8,128]{3,2,1,0:T(8,128)}), f32[12,22,8,128]{3,2,1,0:T(8,128)S(1)}, u32[]{:S(2)}, u32[]{:S(2)}) async-start(f32[12,22,8,128]{3,2,1,0:T(8,128)} %shard_map.37), calls=%async_computation | async-start | bytes 2162688 | tf_op jit(solution)/shard_map/all_to_all | solution.py:215
  26.4 6.1 %copy-start = (f32[22,32,384]{2,1,0:T(8,128)S(1)}, f32[22,32,384]{2,1,0:T(8,128)}, u32[]{:S(2)}) copy-start(f32[22,32,384]{2,1,0:T(8,128)} %variance.3) | copy-start | bytes 3244036
  26.4 25.4 %all-to-all-start.1 = ((f32[12,22,8,128]{3,2,1,0:T(8,128)}), f32[12,22,8,128]{3,2,1,0:T(8,128)S(1)}, u32[]{:S(2)}, u32[]{:S(2)}) async-start(f32[12,22,8,128]{3,2,1,0:T(8,128)} %bitcast.1), calls=%async_computation.1 | async-start | bytes 2162688 | tf_op jit(solution)/shard_map/all_to_all | solution.py:218
  32.8 71.4 %collective-permute-start.6 = (f32[22,8,128]{2,1,0:T(8,128)S(1)}, f32[22,8,128]{2,1,0:T(8,128)S(1)}, u32[]{:S(2)}, u32[]{:S(2)}) collective-permute-start(f32[22,8,128]{2,1,0:T(8,128)S(1)} %get-tuple-element.13), channel_id=1, source_target_pairs={{0,6},{6,12},{12,18},{18,0},{1,7},{7,13},{13,19},{19,1},{2,8},{8,1... | collective-permute-start | bytes 270344 | tf_op jit(solution)/shard_map/ppermute | solution.py:205
  51.8 48.9 %collective-permute-start.3 = (f32[8,22,8,128]{3,2,1,0:T(8,128)S(1)}, f32[8,22,8,128]{3,2,1,0:T(8,128)S(1)}, u32[]{:S(2)}, u32[]{:S(2)}) collective-permute-start(f32[8,22,8,128]{3,2,1,0:T(8,128)S(1)} %slice.9.own), channel_id=1, source_target_pairs={{24,0},{48,24},{72,48},{96,72},{120,96},{144,120},{168,144},{192,1... | collective-permute-start | bytes 2162696 | tf_op jit(solution)/shard_map/ppermute | solution.py:205
  56.4 47.2 %collective-permute-start.2 = (f32[8,22,8,128]{3,2,1,0:T(8,128)S(1)}, f32[8,22,8,128]{3,2,1,0:T(8,128)S(1)}, u32[]{:S(2)}, u32[]{:S(2)}) collective-permute-start(f32[8,22,8,128]{3,2,1,0:T(8,128)S(1)} %slice.9.own), channel_id=1, source_target_pairs={{0,24},{24,48},{48,72},{72,96},{96,120},{120,144},{144,168},{168,1... | collective-permute-start | bytes 2162696 | tf_op jit(solution)/shard_map/ppermute | solution.py:205
  58.4 21.0 %collective-permute-start.1 = (f32[4,22,8,128]{3,2,1,0:T(8,128)S(1)}, f32[4,22,8,128]{3,2,1,0:T(8,128)S(1)}, u32[]{:S(2)}, u32[]{:S(2)}) collective-permute-start(f32[4,22,8,128]{3,2,1,0:T(8,128)S(1)} %slice.8.own), channel_id=1, source_target_pairs={{24,0},{48,24},{72,48},{96,72},{120,96},{144,120},{168,144},{192,1... | collective-permute-start | bytes 1081352 | tf_op jit(solution)/shard_map/ppermute | solution.py:205
  65.7 26.5 %collective-permute-start = (f32[4,22,8,128]{3,2,1,0:T(8,128)S(1)}, f32[4,22,8,128]{3,2,1,0:T(8,128)S(1)}, u32[]{:S(2)}, u32[]{:S(2)}) collective-permute-start(f32[4,22,8,128]{3,2,1,0:T(8,128)S(1)} %slice.8.own), channel_id=1, source_target_pairs={{0,24},{24,48},{48,72},{72,96},{96,120},{120,144},{144,168},{168,1... | collective-permute-start | bytes 1081352 | tf_op jit(solution)/shard_map/ppermute | solution.py:205
  79.4 24.8 %collective-permute-start.7 = (f32[22,8,128]{2,1,0:T(8,128)S(1)}, f32[22,8,128]{2,1,0:T(8,128)S(1)}, u32[]{:S(2)}, u32[]{:S(2)}) collective-permute-start(f32[22,8,128]{2,1,0:T(8,128)S(1)} %get-tuple-element.14), channel_id=1, source_target_pairs={{0,18},{6,0},{12,6},{18,12},{1,19},{7,1},{13,7},{19,13},{2,20},{8,... | collective-permute-start | bytes 270344 | tf_op jit(solution)/shard_map/ppermute | solution.py:205
  92.6 14.9 %collective-permute-start.4 = (f32[22,16,128]{2,1,0:T(8,128)S(1)}, f32[22,16,128]{2,1,0:T(8,128)S(1)}, u32[]{:S(2)}, u32[]{:S(2)}) collective-permute-start(f32[22,16,128]{2,1,0:T(8,128)S(1)} %get-tuple-element.11), channel_id=1, source_target_pairs={{0,6},{6,12},{12,18},{18,0},{1,7},{7,13},{13,19},{19,1},{2,8},{8,1... | collective-permute-start | bytes 540680 | tf_op jit(solution)/shard_map/ppermute | solution.py:205
  100.7 16.8 %collective-permute-start.5 = (f32[22,16,128]{2,1,0:T(8,128)S(1)}, f32[22,16,128]{2,1,0:T(8,128)S(1)}, u32[]{:S(2)}, u32[]{:S(2)}) collective-permute-start(f32[22,16,128]{2,1,0:T(8,128)S(1)} %get-tuple-element.12), channel_id=1, source_target_pairs={{0,18},{6,0},{12,6},{18,12},{1,19},{7,1},{13,7},{19,13},{2,20},{8,... | collective-permute-start | bytes 540680 | tf_op jit(solution)/shard_map/ppermute | solution.py:205
  118.8 17.0 %collective-permute-start.9 = (f32[11,32,384]{2,1,0:T(8,128)S(1)}, f32[11,32,384]{2,1,0:T(8,128)S(1)}, u32[]{:S(2)}, u32[]{:S(2)}) collective-permute-start(f32[11,32,384]{2,1,0:T(8,128)S(1)} %shard_map.42.refs_0_), channel_id=1, source_target_pairs={{24,0},{48,24},{72,48},{96,72},{120,96},{144,120},{168,144},{192,1... | collective-permute-start | bytes 1622024 | tf_op jit(solution)/shard_map/ppermute | solution.py:205
  121.9 20.2 %collective-permute-start.8 = (f32[11,32,384]{2,1,0:T(8,128)S(1)}, f32[11,32,384]{2,1,0:T(8,128)S(1)}, u32[]{:S(2)}, u32[]{:S(2)}) collective-permute-start(f32[11,32,384]{2,1,0:T(8,128)S(1)} %shard_map.42.refs_0_), channel_id=1, source_target_pairs={{0,24},{24,48},{48,72},{72,96},{96,120},{120,144},{144,168},{168,1... | collective-permute-start | bytes 1622024 | tf_op jit(solution)/shard_map/ppermute | solution.py:205
  126.0 20.5 %collective-permute-start.11 = (f32[11,32,384]{2,1,0:T(8,128)S(1)}, f32[11,32,384]{2,1,0:T(8,128)S(1)}, u32[]{:S(2)}, u32[]{:S(2)}) collective-permute-start(f32[11,32,384]{2,1,0:T(8,128)S(1)} %shard_map.43.refs_3_), channel_id=1, source_target_pairs={{24,0},{48,24},{72,48},{96,72},{120,96},{144,120},{168,144},{192,1... | collective-permute-start | bytes 1622024 | tf_op jit(solution)/shard_map/ppermute | solution.py:205
  132.4 19.7 %collective-permute-start.10 = (f32[11,32,384]{2,1,0:T(8,128)S(1)}, f32[11,32,384]{2,1,0:T(8,128)S(1)}, u32[]{:S(2)}, u32[]{:S(2)}) collective-permute-start(f32[11,32,384]{2,1,0:T(8,128)S(1)} %shard_map.43.refs_3_), channel_id=1, source_target_pairs={{0,24},{24,48},{48,72},{72,96},{96,120},{120,144},{144,168},{168,1... | collective-permute-start | bytes 1622024 | tf_op jit(solution)/shard_map/ppermute | solution.py:205

commit v2 on v1

--- a/solution.py
+++ b/solution.py
@@ -14,8 +14,6 @@
 DEVS = 6
 PADDED = 24
 TILE = 128
-CUTS = 2
-PART = LEVELS // CUTS
 
 
 def tap_scale():
@@ -52,21 +50,32 @@
     return jnp.where(tile == 0, edge, jnp.where(tile == 1, first, jnp.where(tile == 2, second, halo)))
 
 
-def wide_column(n):
-    m = n - COLS
-    column = jnp.where(n < COLS, n, jnp.where(m < 64, n, m - TILE))
-    return column, (n < COLS) | (m < HALO) | (m >= TILE - HALO)
-
-
-def lon_matrices():
-    wide = COLS + TILE
-    shape = (wide, wide)
-    out, valid = wide_column(iota(shape, 1))
-    forward = weights(stored_column(iota(shape, 0)) - out, valid)
-    shape = (wide, COLS)
-    held, valid = wide_column(iota(shape, 0))
-    adjoint = weights(held - iota(shape, 1), valid)
-    return split_outside(forward) + split_outside(adjoint)
+def band(column_in, column_out, valid):
+    return split_outside(weights(column_in - column_out, valid))
+
+
+def inner_matrices():
+    shape = (COLS, COLS)
+    outer, inner = iota(shape, 0), iota(shape, 1)
+    forward = band(stored_column(outer), inner, jnp.full(shape, True))
+    shape = (COLS, 2 * TILE)
+    outer, inner = iota(shape, 0), iota(shape, 1)
+    return forward + band(outer, stored_column(inner + TILE), jnp.full(shape, True))
+
+
+def edge_column(n):
+    m = n - 2 * TILE
+    column = jnp.where(n < TILE, n, jnp.where(n < 2 * TILE, n + TILE, jnp.where(m < 64, COLS + m, m - TILE)))
+    return column, (m < HALO) | (m >= TILE - HALO)
+
+
+def edge_matrices():
+    shape = (4 * TILE, 3 * TILE)
+    column, valid = edge_column(iota(shape, 1))
+    forward = band(stored_column(iota(shape, 0)), column, valid)
+    shape = (3 * TILE, TILE)
+    column, valid = edge_column(iota(shape, 0))
+    return forward + band(column, stored_column(iota(shape, 1)), valid)
 
 
 def lat_matrix():
@@ -167,16 +176,24 @@
     to_right[...] = right
 
 
-def lon_body(edge, inner, from_left, from_right, variance, var_left, var_right, fwd_high, fwd_low, adj_high, adj_low, out):
-    flat = (PART * ROWS, TILE)
-    low = iota((PART, 16, TILE), 2) < 64
+def spread_inner_body(edge, inner, variance, fwd_high, fwd_low, adj_high, adj_low, out):
+    count = LEVELS * ROWS
+    held = jnp.concatenate([edge[...].reshape(count, TILE), inner[...].reshape(count, 2 * TILE)], axis=1)
+    smooth = exact_right(held, fwd_high[...], fwd_low[...])
+    scaled = smooth * variance[...].reshape(count, COLS)
+    out[...] = exact_right(scaled, adj_high[...], adj_low[...]).reshape(LEVELS, ROWS, 2 * TILE)
+
+
+def spread_edge_body(edge, inner, from_left, from_right, variance, var_left, var_right, fwd_high, fwd_low, adj_high, adj_low, out):
+    flat = (LEVELS * ROWS, TILE)
+    low = iota((LEVELS, 16, TILE), 2) < 64
     left, right = from_left[...], from_right[...]
     top = jnp.where(low, right, left)
     bottom = pltpu.roll(jnp.where(low, left, right), 64, 2)
     halo = jnp.concatenate([top, bottom], axis=1).reshape(flat)
-    held = jnp.concatenate([edge[...].reshape(flat), inner[...].reshape(PART * ROWS, 2 * TILE), halo], axis=1)
+    held = jnp.concatenate([edge[...].reshape(flat), inner[...].reshape(LEVELS * ROWS, 2 * TILE), halo], axis=1)
     smooth = exact_right(held, fwd_high[...], fwd_low[...])
-    lane = iota((PART, 8, TILE), 2)
+    lane = iota((LEVELS, 8, TILE), 2)
     left, right = var_left[...], var_right[...]
     bands = []
     for band in range(4):
@@ -185,18 +202,29 @@
             l, r = pltpu.roll(left, TILE - HALO * band, 2), pltpu.roll(right, TILE - HALO * band, 2)
         bands.append(jnp.where(lane < HALO, r, jnp.where(lane >= TILE - HALO, l, 0.0)))
     side = jnp.concatenate(bands, axis=1).reshape(flat)
-    scale = jnp.concatenate([variance[...].reshape(PART * ROWS, COLS), side], axis=1)
-    out[...] = exact_right(smooth * scale, adj_high[...], adj_low[...]).reshape(PART, ROWS, COLS)
-
-
-def last_body(matrix, *refs):
-    stacked = matrix[...]
-    out = refs[-1]
-    for part in range(CUTS):
-        own, above, below = refs[3 * part : 3 * part + 3]
-        for level in range(PART):
-            cells = jnp.concatenate([above[level], own[level], below[level]], axis=0)
-            out[part * PART + level] = exact_left(stacked, cells)
+    first, last = variance[:, :, :TILE].reshape(flat), variance[:, :, 2 * TILE :].reshape(flat)
+    scaled = smooth * jnp.concatenate([first, last, side], axis=1)
+    out[...] = exact_right(scaled, adj_high[...], adj_low[...]).reshape(LEVELS, ROWS, TILE)
+
+
+def last_inner_body(matrix, own, above, below, out):
+    stacked = matrix[...]
+    for level in range(LEVELS):
+        out[level] = exact_left(stacked, jnp.concatenate([above[level], own[level], below[level]], axis=0))
+
+
+def last_edge_body(matrix, own, above, below, inner, out):
+    stacked = matrix[...]
+    low = iota((ROWS, TILE), 1) < 64
+    for level in range(0, LEVELS, 2):
+        pair = [jnp.concatenate([above[k], own[k], below[k]], axis=0) for k in (level, level + 1)]
+        done = exact_left(stacked, jnp.concatenate(pair, axis=1))
+        for k in range(2):
+            edge = done[:, TILE * k : TILE * k + TILE]
+            first, second = inner[level + k, :, :TILE], inner[level + k, :, TILE:]
+            out[level + k, :, :TILE] = jnp.where(low, edge, first)
+            out[level + k, :, TILE : 2 * TILE] = jnp.where(low, first, second)
+            out[level + k, :, 2 * TILE :] = jnp.where(low, second, edge)
 
 
 def shifted(cells, axis, step, closed):
@@ -207,7 +235,6 @@
 
 def steps(gradient, vertical, variance):
     lat = lat_matrix()
-    lon = lon_matrices()
     tiles = (2 * DEVS, LEVELS, 8, TILE)
     flat = (2 * DEVS * LEVELS * 8, TILE)
     matrix = jnp.pad(vertical.reshape(DEVS, LEVELS, DEVS, LEVELS), ((0, 0), (0, PADDED - LEVELS)) * 2).reshape(DEVS * PADDED, DEVS * PADDED)
@@ -229,19 +256,13 @@
     var_left, var_right = shifted(to_right, "lon", 1, True), shifted(to_left, "lon", -1, True)
     inner = call(inner_body, f32(LEVELS, ROWS, 2 * TILE))(lat, inner, inner_above, inner_below)
 
-    operands = []
-    for cut in range(CUTS):
-        def block(array, cut=cut):
-            return pl.BlockSpec((PART,) + array.shape[1:], lambda i: (cut, 0, 0))
-
-        arrays = (edge, inner, from_left, from_right, variance, var_left, var_right)
-        specs = [block(a) for a in arrays] + [pl.BlockSpec(m.shape, lambda i: (0, 0)) for m in lon]
-        spread = call(
-            lon_body, f32(PART, ROWS, COLS), grid=(1,), in_specs=specs,
-            out_specs=pl.BlockSpec((PART, ROWS, COLS), lambda i: (0, 0, 0)),
-        )(*arrays, *lon)
-        operands += [spread, shifted(spread, "lat", 1, False), shifted(spread, "lat", -1, False)]
-    return call(last_body, f32(LEVELS, ROWS, COLS))(lat, *operands)
+    back = call(spread_inner_body, f32(LEVELS, ROWS, 2 * TILE))(edge, inner, variance, *inner_matrices())
+    back_above, back_below = shifted(back, "lat", 1, False), shifted(back, "lat", -1, False)
+    sides = (from_left, from_right, variance, var_left, var_right)
+    rim = call(spread_edge_body, f32(LEVELS, ROWS, TILE))(edge, inner, *sides, *edge_matrices())
+    rim_above, rim_below = shifted(rim, "lat", 1, False), shifted(rim, "lat", -1, False)
+    back = call(last_inner_body, f32(LEVELS, ROWS, 2 * TILE))(lat, back, back_above, back_below)
+    return call(last_edge_body, f32(LEVELS, ROWS, COLS))(lat, rim, rim_above, rim_below, back)
 
 
 def solution(mesh):

time: 154 us -> 151 us (0.981)
  the two profiles are of different devices: /device:TPU:96 before, /device:TPU:94 now
where the time goes in v2:
time: 151 us; the launch traced here: 150 us
  starting transfers between devices  78.4 us (52%)
  waiting for transfers between devices  56.9 us (38%)
  Pallas kernels  10.3 us (7%)
  other arithmetic  2.66 us (2%)
  local copies, waits for them, and re-layouts  1.7 us (1%)
    ppermute x12, starting transfers between devices, shifted(): return lax.ppermute(cells, axis, pairs)  67.1 us
    ppermute x12, waiting for transfers between devices, shifted(): return lax.ppermute(cells, axis, pairs)  33.2 us
    all_to_all x1, waiting for transfers between devices, steps(): gathered = lax.all_to_all(packed, 'lev', 0, 0, tiled=True)  16.7 us
    all_to_all x1, waiting for transfers between devices, steps(): mixed = lax.all_to_all(mixed, 'lev', 0, 0, tiled=True)  7.07 us
    all_to_all x1, starting transfers between devices, steps(): mixed = lax.all_to_all(mixed, 'lev', 0, 0, tiled=True)  6.12 us
    all_to_all x1, starting transfers between devices, steps(): gathered = lax.all_to_all(packed, 'lev', 0, 0, tiled=True)  5.23 us
  transfers between devices with their start and end apart: 14, of which 7 were waited for; matrix products, arithmetic and copies ran while one was open for 2% of the time, Pallas kernels for 4%

profile of v2, /device:TPU:94, one launch (start us, length us, event | category | flops | bytes accessed | tf_op | source)
XLA Modules:
  0.0 150.4 jit_solution(445976192157745458)
XLA Ops:
  0.0 0.0 copy-start.1
  0.0 1.2 copy-done.1
  1.2 1.1 shard_map.37
  2.3 0.0 copy-start.2
  2.3 5.2 %all-to-all-start = ((f32[12,22,8,128]{3,2,1,0:T(8,128)}), f32[12,22,8,128]{3,2,1,0:T(8,128)S(1)}, u32[]{:S(2)}, u32[]{:S(2)}) async-start(f32[12,22,8,128]{3,2,1,0:T(8,128)} %shard_map.37), calls=%async_computation | async-start | bytes 2162688 | tf_op jit(solution)/shard_map/all_to_all | solution.py:242
  7.5 0.0 copy-done.2
  7.5 0.2 reshape.12
  7.8 0.2 reshape.13.matrix
  7.9 16.7 %all-to-all-done = f32[12,22,8,128]{3,2,1,0:T(8,128)S(1)} async-done(((f32[12,22,8,128]{3,2,1,0:T(8,128)}), f32[12,22,8,128]{3,2,1,0:T(8,128)S(1)}, u32[]{:S(2)}, u32[]{:S(2)}) %all-to-all-start) | async-done | bytes 1081376 | tf_op jit(solution)/shard_map/all_to_all | solution.py:242
  24.6 1.8 %shard_map.38 = f32[2112,128]{1,0:T(8,128)} custom-call(f32[144,144]{1,0:T(8,128)S(1)} %reshape.13.matrix, f32[2112,128]{1,0:T(8,128)S(1)} %bitcast.2), custom_call_target="tpu_custom_call" | custom-call | tf_op jit(solution)/shard_map/pallas_call | solution.py:244
  26.4 6.1 %all-to-all-start.1 = ((f32[12,22,8,128]{3,2,1,0:T(8,128)}), f32[12,22,8,128]{3,2,1,0:T(8,128)S(1)}, u32[]{:S(2)}, u32[]{:S(2)}) async-start(f32[12,22,8,128]{3,2,1,0:T(8,128)} %bitcast.1), calls=%async_computation.1 | async-start | bytes 2162688 | tf_op jit(solution)/shard_map/all_to_all | solution.py:245
  32.6 0.0 copy-done
  32.6 0.2 shard_map.41
  32.8 11.5 %collective-permute-start.6 = (f32[22,8,128]{2,1,0:T(8,128)S(1)}, f32[22,8,128]{2,1,0:T(8,128)S(1)}, u32[]{:S(2)}, u32[]{:S(2)}) collective-permute-start(f32[22,8,128]{2,1,0:T(8,128)S(1)} %get-tuple-element.13), channel_id=1, source_target_pairs={{0,6},{6,12},{12,18},{18,0},{1,7},{7,13},{13,19},{19,1},{2,8},{8,1... | collective-permute-start | bytes 270344 | tf_op jit(solution)/shard_map/ppermute | solution.py:233
  44.5 0.2 fusion.21
  44.7 7.1 %all-to-all-done.1 = f32[12,22,8,128]{3,2,1,0:T(8,128)S(1)} async-done(((f32[12,22,8,128]{3,2,1,0:T(8,128)}), f32[12,22,8,128]{3,2,1,0:T(8,128)S(1)}, u32[]{:S(2)}, u32[]{:S(2)}) %all-to-all-start.1) | async-done | bytes 1081376 | tf_op jit(solution)/shard_map/all_to_all | solution.py:245
  51.8 4.6 %collective-permute-start.2 = (f32[8,22,8,128]{3,2,1,0:T(8,128)S(1)}, f32[8,22,8,128]{3,2,1,0:T(8,128)S(1)}, u32[]{:S(2)}, u32[]{:S(2)}) collective-permute-start(f32[8,22,8,128]{3,2,1,0:T(8,128)S(1)} %slice.9.own), channel_id=1, source_target_pairs={{0,24},{24,48},{48,72},{72,96},{96,120},{120,144},{144,168},{168,1... | collective-permute-start | bytes 2162696 | tf_op jit(solution)/shard_map/ppermute | solution.py:233
  56.5 1.9 %collective-permute-start.3 = (f32[8,22,8,128]{3,2,1,0:T(8,128)S(1)}, f32[8,22,8,128]{3,2,1,0:T(8,128)S(1)}, u32[]{:S(2)}, u32[]{:S(2)}) collective-permute-start(f32[8,22,8,128]{3,2,1,0:T(8,128)S(1)} %slice.9.own), channel_id=1, source_target_pairs={{24,0},{48,24},{72,48},{96,72},{120,96},{144,120},{168,144},{192,1... | collective-permute-start | bytes 2162696 | tf_op jit(solution)/shard_map/ppermute | solution.py:233
  58.4 0.7 fusion.14
  59.2 7.2 %collective-permute-start = (f32[4,22,8,128]{3,2,1,0:T(8,128)S(1)}, f32[4,22,8,128]{3,2,1,0:T(8,128)S(1)}, u32[]{:S(2)}, u32[]{:S(2)}) collective-permute-start(f32[4,22,8,128]{3,2,1,0:T(8,128)S(1)} %slice.8.own), channel_id=1, source_target_pairs={{0,24},{24,48},{48,72},{72,96},{96,120},{120,144},{144,168},{168,1... | collective-permute-start | bytes 1081352 | tf_op jit(solution)/shard_map/ppermute | solution.py:233
  66.4 1.9 %collective-permute-start.1 = (f32[4,22,8,128]{3,2,1,0:T(8,128)S(1)}, f32[4,22,8,128]{3,2,1,0:T(8,128)S(1)}, u32[]{:S(2)}, u32[]{:S(2)}) collective-permute-start(f32[4,22,8,128]{3,2,1,0:T(8,128)S(1)} %slice.8.own), channel_id=1, source_target_pairs={{24,0},{48,24},{72,48},{96,72},{120,96},{144,120},{168,144},{192,1... | collective-permute-start | bytes 1081352 | tf_op jit(solution)/shard_map/ppermute | solution.py:233
  68.4 1.0 fusion.7
  69.4 10.1 %collective-permute-done.above = f32[4,22,8,128]{3,2,1,0:T(8,128)S(1)} collective-permute-done((f32[4,22,8,128]{3,2,1,0:T(8,128)S(1)}, f32[4,22,8,128]{3,2,1,0:T(8,128)S(1)}, u32[]{:S(2)}, u32[]{:S(2)}) %collective-permute-start) | collective-permute-done | bytes 360480 | tf_op jit(solution)/shard_map/ppermute | solution.py:233
  79.4 12.8 %collective-permute-start.7 = (f32[22,8,128]{2,1,0:T(8,128)S(1)}, f32[22,8,128]{2,1,0:T(8,128)S(1)}, u32[]{:S(2)}, u32[]{:S(2)}) collective-permute-start(f32[22,8,128]{2,1,0:T(8,128)S(1)} %get-tuple-element.14), channel_id=1, source_target_pairs={{0,18},{6,0},{12,6},{18,12},{1,19},{7,1},{13,7},{19,13},{2,20},{8,... | collective-permute-start | bytes 270344 | tf_op jit(solution)/shard_map/ppermute | solution.py:233
  92.2 0.0 collective-permute-done.1.below
  92.2 0.4 shard_map.39
  92.6 0.0 collective-permute-done.2.above
  92.6 0.0 collective-permute-done.3.below
  92.6 0.5 shard_map.40.inner
  93.2 2.8 %shard_map.43.own = f32[22,32,256]{2,1,0:T(8,128)S(1)} custom-call(f32[22,32,128]{2,1,0:T(8,128)S(1)} %get-tuple-element.10.edge, f32[22,32,256]{2,1,0:T(8,128)S(1)} %shard_map.40.inner, f32[22,32,384]{2,1,0:T(8,128)S(1)} %copy-done, bf16[384,384]{1,0:T(8,128)(2,1)S(1)} %get-tuple-element.18.fwd_high, bf16[384,384]{1,0:T(8,128)(2,1)S(1)} %get-tuple-element.17.fwd_low, ...), custom_call_target="tpu_custom_call" | custom-call | tf_op jit(solution)/shard_map/pallas_call | solution.py:259
  95.9 7.7 %collective-permute-start.10 = (f32[22,32,256]{2,1,0:T(8,128)S(1)}, f32[22,32,256]{2,1,0:T(8,128)S(1)}, u32[]{:S(2)}, u32[]{:S(2)}) collective-permute-start(f32[22,32,256]{2,1,0:T(8,128)S(1)} %shard_map.43.own), channel_id=1, source_target_pairs={{0,24},{24,48},{48,72},{72,96},{96,120},{120,144},{144,168},{168,1... | collective-permute-start | bytes 2162696 | tf_op jit(solution)/shard_map/ppermute | solution.py:233
  103.6 1.9 %collective-permute-start.11 = (f32[22,32,256]{2,1,0:T(8,128)S(1)}, f32[22,32,256]{2,1,0:T(8,128)S(1)}, u32[]{:S(2)}, u32[]{:S(2)}) collective-permute-start(f32[22,32,256]{2,1,0:T(8,128)S(1)} %shard_map.43.own), channel_id=1, source_target_pairs={{24,0},{48,24},{72,48},{96,72},{120,96},{144,120},{168,144},{192,1... | collective-permute-start | bytes 2162696 | tf_op jit(solution)/shard_map/ppermute | solution.py:233
  105.6 4.3 %collective-permute-start.4 = (f32[22,16,128]{2,1,0:T(8,128)S(1)}, f32[22,16,128]{2,1,0:T(8,128)S(1)}, u32[]{:S(2)}, u32[]{:S(2)}) collective-permute-start(f32[22,16,128]{2,1,0:T(8,128)S(1)} %get-tuple-element.11), channel_id=1, source_target_pairs={{0,6},{6,12},{12,18},{18,0},{1,7},{7,13},{13,19},{19,1},{2,8},{8,1... | collective-permute-start | bytes 540680 | tf_op jit(solution)/shard_map/ppermute | solution.py:233
  109.9 0.0 collective-permute-done.6.var_left
  109.9 4.5 %collective-permute-start.5 = (f32[22,16,128]{2,1,0:T(8,128)S(1)}, f32[22,16,128]{2,1,0:T(8,128)S(1)}, u32[]{:S(2)}, u32[]{:S(2)}) collective-permute-start(f32[22,16,128]{2,1,0:T(8,128)S(1)} %get-tuple-element.12), channel_id=1, source_target_pairs={{0,18},{6,0},{12,6},{18,12},{1,19},{7,1},{13,7},{19,13},{2,20},{8,... | collective-permute-start | bytes 540680 | tf_op jit(solution)/shard_map/ppermute | solution.py:233
  114.5 0.6 fusion.28
  115.1 0.0 collective-permute-done.7.var_right
  115.1 7.1 %collective-permute-done.4.from_left = f32[22,16,128]{2,1,0:T(8,128)S(1)} collective-permute-done((f32[22,16,128]{2,1,0:T(8,128)S(1)}, f32[22,16,128]{2,1,0:T(8,128)S(1)}, u32[]{:S(2)}, u32[]{:S(2)}) %collective-permute-start.4) | collective-permute-done | bytes 180256 | tf_op jit(solution)/shard_map/ppermute | solution.py:233
  122.2 3.7 %collective-permute-done.5.from_right = f32[22,16,128]{2,1,0:T(8,128)S(1)} collective-permute-done((f32[22,16,128]{2,1,0:T(8,128)S(1)}, f32[22,16,128]{2,1,0:T(8,128)S(1)}, u32[]{:S(2)}, u32[]{:S(2)}) %collective-permute-start.5) | collective-permute-done | bytes 180256 | tf_op jit(solution)/shard_map/ppermute | solution.py:233
  125.9 1.7 %shard_map.42.own = f32[22,32,128]{2,1,0:T(8,128)S(1)} custom-call(f32[22,32,128]{2,1,0:T(8,128)S(1)} %get-tuple-element.10.edge, f32[22,32,256]{2,1,0:T(8,128)S(1)} %shard_map.40.inner, f32[22,16,128]{2,1,0:T(8,128)S(1)} %collective-permute-done.4.from_left, f32[22,16,128]{2,1,0:T(8,128)S(1)} %collective-permute-done.5.from_right, ...), custom_call_target="tpu_custom_call" | custom-call | tf_op jit(solution)/shard_map/pallas_call | solution.py:262
  127.6 6.7 %collective-permute-start.8 = (f32[22,32,128]{2,1,0:T(8,128)S(1)}, f32[22,32,128]{2,1,0:T(8,128)S(1)}, u32[]{:S(2)}, u32[]{:S(2)}) collective-permute-start(f32[22,32,128]{2,1,0:T(8,128)S(1)} %shard_map.42.own), channel_id=1, source_target_pairs={{0,24},{24,48},{48,72},{72,96},{96,120},{120,144},{144,168},{168,1... | collective-permute-start | bytes 1081352 | tf_op jit(solution)/shard_map/ppermute | solution.py:233
  134.3 1.9 %collective-permute-start.9 = (f32[22,32,128]{2,1,0:T(8,128)S(1)}, f32[22,32,128]{2,1,0:T(8,128)S(1)}, u32[]{:S(2)}, u32[]{:S(2)}) collective-permute-start(f32[22,32,128]{2,1,0:T(8,128)S(1)} %shard_map.42.own), channel_id=1, source_target_pairs={{24,0},{48,24},{72,48},{96,72},{120,96},{144,120},{168,144},{192,1... | collective-permute-start | bytes 1081352 | tf_op jit(solution)/shard_map/ppermute | solution.py:233
  136.3 0.0 collective-permute-done.10.above
  136.3 0.0 collective-permute-done.11.below
  136.3 0.5 shard_map.44.inner
  136.8 4.8 %collective-permute-done.8.above = f32[22,32,128]{2,1,0:T(8,128)S(1)} collective-permute-done((f32[22,32,128]{2,1,0:T(8,128)S(1)}, f32[22,32,128]{2,1,0:T(8,128)S(1)}, u32[]{:S(2)}, u32[]{:S(2)}) %collective-permute-start.8) | collective-permute-done | bytes 360480 | tf_op jit(solution)/shard_map/ppermute | solution.py:233
  141.6 7.4 %collective-permute-done.9.below = f32[22,32,128]{2,1,0:T(8,128)S(1)} collective-permute-done((f32[22,32,128]{2,1,0:T(8,128)S(1)}, f32[22,32,128]{2,1,0:T(8,128)S(1)}, u32[]{:S(2)}, u32[]{:S(2)}) %collective-permute-start.9) | collective-permute-done | bytes 360480 | tf_op jit(solution)/shard_map/ppermute | solution.py:233
  149.1 1.3 shard_map.45
  (21 shorter events, 0.2 us)
Async XLA Ops:
  0.0 1.2 copy-start.1
  2.3 5.2 %copy-start.2 = (f32[132,132]{1,0:T(8,128)S(1)}, f32[132,132]{1,0:T(8,128)}, u32[]{:S(2)}) copy-start(f32[132,132]{1,0:T(8,128)} %param.4) | copy-start | bytes 209092
  2.3 22.3 %all-to-all-start = ((f32[12,22,8,128]{3,2,1,0:T(8,128)}), f32[12,22,8,128]{3,2,1,0:T(8,128)S(1)}, u32[]{:S(2)}, u32[]{:S(2)}) async-start(f32[12,22,8,128]{3,2,1,0:T(8,128)} %shard_map.37), calls=%async_computation | async-start | bytes 2162688 | tf_op jit(solution)/shard_map/all_to_all | solution.py:242
  26.4 6.1 %copy-start = (f32[22,32,384]{2,1,0:T(8,128)S(1)}, f32[22,32,384]{2,1,0:T(8,128)}, u32[]{:S(2)}) copy-start(f32[22,32,384]{2,1,0:T(8,128)} %variance.3) | copy-start | bytes 3244036
  26.4 25.4 %all-to-all-start.1 = ((f32[12,22,8,128]{3,2,1,0:T(8,128)}), f32[12,22,8,128]{3,2,1,0:T(8,128)S(1)}, u32[]{:S(2)}, u32[]{:S(2)}) async-start(f32[12,22,8,128]{3,2,1,0:T(8,128)} %bitcast.1), calls=%async_computation.1 | async-start | bytes 2162688 | tf_op jit(solution)/shard_map/all_to_all | solution.py:245
  32.8 77.1 %collective-permute-start.6 = (f32[22,8,128]{2,1,0:T(8,128)S(1)}, f32[22,8,128]{2,1,0:T(8,128)S(1)}, u32[]{:S(2)}, u32[]{:S(2)}) collective-permute-start(f32[22,8,128]{2,1,0:T(8,128)S(1)} %get-tuple-element.13), channel_id=1, source_target_pairs={{0,6},{6,12},{12,18},{18,0},{1,7},{7,13},{13,19},{19,1},{2,8},{8,1... | collective-permute-start | bytes 270344 | tf_op jit(solution)/shard_map/ppermute | solution.py:233
  51.8 40.8 %collective-permute-start.2 = (f32[8,22,8,128]{3,2,1,0:T(8,128)S(1)}, f32[8,22,8,128]{3,2,1,0:T(8,128)S(1)}, u32[]{:S(2)}, u32[]{:S(2)}) collective-permute-start(f32[8,22,8,128]{3,2,1,0:T(8,128)S(1)} %slice.9.own), channel_id=1, source_target_pairs={{0,24},{24,48},{48,72},{72,96},{96,120},{120,144},{144,168},{168,1... | collective-permute-start | bytes 2162696 | tf_op jit(solution)/shard_map/ppermute | solution.py:233
  56.5 36.2 %collective-permute-start.3 = (f32[8,22,8,128]{3,2,1,0:T(8,128)S(1)}, f32[8,22,8,128]{3,2,1,0:T(8,128)S(1)}, u32[]{:S(2)}, u32[]{:S(2)}) collective-permute-start(f32[8,22,8,128]{3,2,1,0:T(8,128)S(1)} %slice.9.own), channel_id=1, source_target_pairs={{24,0},{48,24},{72,48},{96,72},{120,96},{144,120},{168,144},{192,1... | collective-permute-start | bytes 2162696 | tf_op jit(solution)/shard_map/ppermute | solution.py:233
  59.2 20.3 %collective-permute-start = (f32[4,22,8,128]{3,2,1,0:T(8,128)S(1)}, f32[4,22,8,128]{3,2,1,0:T(8,128)S(1)}, u32[]{:S(2)}, u32[]{:S(2)}) collective-permute-start(f32[4,22,8,128]{3,2,1,0:T(8,128)S(1)} %slice.8.own), channel_id=1, source_target_pairs={{0,24},{24,48},{48,72},{72,96},{96,120},{120,144},{144,168},{168,1... | collective-permute-start | bytes 1081352 | tf_op jit(solution)/shard_map/ppermute | solution.py:233
  66.4 25.8 %collective-permute-start.1 = (f32[4,22,8,128]{3,2,1,0:T(8,128)S(1)}, f32[4,22,8,128]{3,2,1,0:T(8,128)S(1)}, u32[]{:S(2)}, u32[]{:S(2)}) collective-permute-start(f32[4,22,8,128]{3,2,1,0:T(8,128)S(1)} %slice.8.own), channel_id=1, source_target_pairs={{24,0},{48,24},{72,48},{96,72},{120,96},{144,120},{168,144},{192,1... | collective-permute-start | bytes 1081352 | tf_op jit(solution)/shard_map/ppermute | solution.py:233
  79.4 35.6 %collective-permute-start.7 = (f32[22,8,128]{2,1,0:T(8,128)S(1)}, f32[22,8,128]{2,1,0:T(8,128)S(1)}, u32[]{:S(2)}, u32[]{:S(2)}) collective-permute-start(f32[22,8,128]{2,1,0:T(8,128)S(1)} %get-tuple-element.14), channel_id=1, source_target_pairs={{0,18},{6,0},{12,6},{18,12},{1,19},{7,1},{13,7},{19,13},{2,20},{8,... | collective-permute-start | bytes 270344 | tf_op jit(solution)/shard_map/ppermute | solution.py:233
  95.9 40.3 %collective-permute-start.10 = (f32[22,32,256]{2,1,0:T(8,128)S(1)}, f32[22,32,256]{2,1,0:T(8,128)S(1)}, u32[]{:S(2)}, u32[]{:S(2)}) collective-permute-start(f32[22,32,256]{2,1,0:T(8,128)S(1)} %shard_map.43.own), channel_id=1, source_target_pairs={{0,24},{24,48},{48,72},{72,96},{96,120},{120,144},{144,168},{168,1... | collective-permute-start | bytes 2162696 | tf_op jit(solution)/shard_map/ppermute | solution.py:233
  103.6 32.6 %collective-permute-start.11 = (f32[22,32,256]{2,1,0:T(8,128)S(1)}, f32[22,32,256]{2,1,0:T(8,128)S(1)}, u32[]{:S(2)}, u32[]{:S(2)}) collective-permute-start(f32[22,32,256]{2,1,0:T(8,128)S(1)} %shard_map.43.own), channel_id=1, source_target_pairs={{24,0},{48,24},{72,48},{96,72},{120,96},{144,120},{168,144},{192,1... | collective-permute-start | bytes 2162696 | tf_op jit(solution)/shard_map/ppermute | solution.py:233
  105.6 16.6 %collective-permute-start.4 = (f32[22,16,128]{2,1,0:T(8,128)S(1)}, f32[22,16,128]{2,1,0:T(8,128)S(1)}, u32[]{:S(2)}, u32[]{:S(2)}) collective-permute-start(f32[22,16,128]{2,1,0:T(8,128)S(1)} %get-tuple-element.11), channel_id=1, source_target_pairs={{0,6},{6,12},{12,18},{18,0},{1,7},{7,13},{13,19},{19,1},{2,8},{8,1... | collective-permute-start | bytes 540680 | tf_op jit(solution)/shard_map/ppermute | solution.py:233
  109.9 16.0 %collective-permute-start.5 = (f32[22,16,128]{2,1,0:T(8,128)S(1)}, f32[22,16,128]{2,1,0:T(8,128)S(1)}, u32[]{:S(2)}, u32[]{:S(2)}) collective-permute-start(f32[22,16,128]{2,1,0:T(8,128)S(1)} %get-tuple-element.12), channel_id=1, source_target_pairs={{0,18},{6,0},{12,6},{18,12},{1,19},{7,1},{13,7},{19,13},{2,20},{8,... | collective-permute-start | bytes 540680 | tf_op jit(solution)/shard_map/ppermute | solution.py:233
  127.6 14.0 %collective-permute-start.8 = (f32[22,32,128]{2,1,0:T(8,128)S(1)}, f32[22,32,128]{2,1,0:T(8,128)S(1)}, u32[]{:S(2)}, u32[]{:S(2)}) collective-permute-start(f32[22,32,128]{2,1,0:T(8,128)S(1)} %shard_map.42.own), channel_id=1, source_target_pairs={{0,24},{24,48},{48,72},{72,96},{96,120},{120,144},{144,168},{168,1... | collective-permute-start | bytes 1081352 | tf_op jit(solution)/shard_map/ppermute | solution.py:233
  134.3 14.7 %collective-permute-start.9 = (f32[22,32,128]{2,1,0:T(8,128)S(1)}, f32[22,32,128]{2,1,0:T(8,128)S(1)}, u32[]{:S(2)}, u32[]{:S(2)}) collective-permute-start(f32[22,32,128]{2,1,0:T(8,128)S(1)} %shard_map.42.own), channel_id=1, source_target_pairs={{24,0},{48,24},{72,48},{96,72},{120,96},{144,120},{168,144},{192,1... | collective-permute-start | bytes 1081352 | tf_op jit(solution)/shard_map/ppermute | solution.py:233

commit v3 on v2

--- a/solution.py
+++ b/solution.py
@@ -23,12 +23,7 @@
 
 def weights(offset, valid):
     values = jnp.exp(-0.5 * (offset.astype(jnp.float32) * (2.0 / HALO)) ** 2) * tap_scale()
-    return jnp.where(valid & (jnp.abs(offset) <= HALO), values, 0.0)
-
-
-def split_outside(values):
-    high = lax.reduce_precision(values, 8, 7)
-    return high.astype(jnp.bfloat16), (values - high).astype(jnp.bfloat16)
+    return jnp.where(valid, values, 0.0)
 
 
 def split(values):
@@ -41,7 +36,7 @@
 
 
 def stored_column(k):
-    tile, lane = k // TILE, k % TILE
+    tile, lane = k >> 7, k & (TILE - 1)
     low = lane < 64
     edge = jnp.where(low, lane, 256 + lane)
     first = jnp.where(low, 128 + lane, lane)
@@ -50,38 +45,33 @@
     return jnp.where(tile == 0, edge, jnp.where(tile == 1, first, jnp.where(tile == 2, second, halo)))
 
 
-def band(column_in, column_out, valid):
-    return split_outside(weights(column_in - column_out, valid))
-
-
-def inner_matrices():
-    shape = (COLS, COLS)
-    outer, inner = iota(shape, 0), iota(shape, 1)
-    forward = band(stored_column(outer), inner, jnp.full(shape, True))
-    shape = (COLS, 2 * TILE)
-    outer, inner = iota(shape, 0), iota(shape, 1)
-    return forward + band(outer, stored_column(inner + TILE), jnp.full(shape, True))
-
-
 def edge_column(n):
     m = n - 2 * TILE
     column = jnp.where(n < TILE, n, jnp.where(n < 2 * TILE, n + TILE, jnp.where(m < 64, COLS + m, m - TILE)))
     return column, (m < HALO) | (m >= TILE - HALO)
 
 
-def edge_matrices():
-    shape = (4 * TILE, 3 * TILE)
-    column, valid = edge_column(iota(shape, 1))
-    forward = band(stored_column(iota(shape, 0)), column, valid)
-    shape = (3 * TILE, TILE)
-    column, valid = edge_column(iota(shape, 0))
-    return forward + band(column, stored_column(iota(shape, 1)), valid)
-
-
-def lat_matrix():
+MATRICES = ((COLS, COLS), (COLS, 2 * TILE), (4 * TILE, 3 * TILE), (3 * TILE, TILE))
+
+
+def matrices_body(lat, *outs):
     shape = (ROWS, 3 * ROWS)
-    high, low = split_outside(weights(iota(shape, 1) - iota(shape, 0) - ROWS, jnp.full(shape, True)))
-    return jnp.concatenate([high, low], axis=0)
+    offset = iota(shape, 1) - iota(shape, 0) - ROWS
+    lat[...] = jnp.concatenate(split(weights(offset, jnp.abs(offset) <= HALO)), axis=0)
+    for kind, shape in enumerate(MATRICES):
+        outer, inner = iota(shape, 0), iota(shape, 1)
+        valid = True
+        if kind == 0:
+            offset = stored_column(outer) - inner
+        elif kind == 1:
+            offset = outer - stored_column(inner + TILE)
+        elif kind == 2:
+            column, valid = edge_column(inner)
+            offset = stored_column(outer) - column
+        else:
+            column, valid = edge_column(outer)
+            offset = column - stored_column(inner)
+        outs[2 * kind][...], outs[2 * kind + 1][...] = split(weights(offset, (jnp.abs(offset) <= HALO) & valid))
 
 
 def dot(a, b):
@@ -101,7 +91,7 @@
 
 
 def call(body, out_shape, **kwargs):
-    return pl.pallas_call(body, out_shape=out_shape, compiler_params=pltpu.CompilerParams(vmem_limit_bytes=48 * 2**20), **kwargs)
+    return pl.pallas_call(body, out_shape=out_shape, compiler_params=pltpu.CompilerParams(vmem_limit_bytes=20 * 2**20), **kwargs)
 
 
 def f32(*shape):
@@ -112,26 +102,28 @@
     low = iota((LEVELS, 8, TILE), 2) < 64
     for band in range(4):
         t0, t1, t2 = (field[:, 8 * band : 8 * band + 8, TILE * k : TILE * k + TILE] for k in range(3))
-        out[band] = jnp.where(low, t0, t2)
-        out[4 + band] = jnp.where(low, t1, t0)
-        out[8 + band] = jnp.where(low, t2, t1)
-
-
-def mix_body(matrix, field, out, cells):
-    high, low = split(matrix[...])
-    cells[...] = jnp.zeros_like(cells)
-    for piece in range(DEVS):
-        for tile in range(2):
+        tiles = (jnp.where(low, t0, t2), jnp.where(low, t1, t0), jnp.where(low, t2, t1))
+        for kind in range(3):
+            half, dev = divmod(4 * kind + band, DEVS)
+            out[2 * dev + half] = tiles[kind]
+
+
+def mix_half(half):
+    def body(matrix, field, out, cells):
+        high, low = split(matrix[...])
+        cells[...] = jnp.zeros_like(cells)
+        for piece in range(DEVS):
             for row in range(8):
-                place = pl.ds((2 * piece + tile) * LEVELS * 8 + row, LEVELS, stride=8)
-                cells[PADDED * piece : PADDED * piece + LEVELS, pl.ds((8 * tile + row) * TILE, TILE)] = field[place, :]
-    for tile in range(2):
-        cells_high, cells_low = split(cells[:, 8 * TILE * tile : 8 * TILE * (tile + 1)])
+                place = pl.ds((2 * piece + half) * LEVELS * 8 + row, LEVELS, stride=8)
+                cells[PADDED * piece : PADDED * piece + LEVELS, TILE * row : TILE * row + TILE] = field[place, :]
+        cells_high, cells_low = split(cells[...])
         mixed = dot(high, cells_high) + dot(low, cells_high) + dot(high, cells_low)
         for piece in range(DEVS):
             for row in range(8):
-                place = pl.ds((2 * piece + tile) * LEVELS * 8 + row, LEVELS, stride=8)
+                place = pl.ds(piece * LEVELS * 8 + row, LEVELS, stride=8)
                 out[place, :] = mixed[PADDED * piece : PADDED * piece + LEVELS, TILE * row : TILE * row + TILE]
+
+    return body
 
 
 def edge_body(matrix, own, above, below, out, to_left, to_right):
@@ -151,13 +143,16 @@
             to_right[level + k] = jnp.where(low, bottom, top)
 
 
-def inner_body(matrix, own, above, below, out):
-    stacked = matrix[...]
+def inner_body(matrix, *refs):
+    stacked, out = matrix[...], refs[-1]
+    early, late = refs[:3], refs[3:6]
+
+    def column(side, tile, level):
+        places = [4 * (tile + 1) + band for band in range(4)]
+        return [early[side][p, level] if p < DEVS else late[side][p - DEVS, level] for p in places]
+
     for level in range(LEVELS):
-        sides = [
-            jnp.concatenate([ref[4 * tile + band, level] for ref in (above, own, below) for band in range(4)], axis=0)
-            for tile in range(2)
-        ]
+        sides = [jnp.concatenate([c for side in (1, 0, 2) for c in column(side, tile, level)], axis=0) for tile in range(2)]
         out[level] = exact_left(stacked, jnp.concatenate(sides, axis=1))
 
 
@@ -234,32 +229,33 @@
 
 
 def steps(gradient, vertical, variance):
-    lat = lat_matrix()
+    shapes = [(2 * ROWS, 3 * ROWS)] + [shape for shape in MATRICES for _ in range(2)]
+    lat, *bands = call(matrices_body, [jax.ShapeDtypeStruct(shape, jnp.bfloat16) for shape in shapes])()
     tiles = (2 * DEVS, LEVELS, 8, TILE)
     flat = (2 * DEVS * LEVELS * 8, TILE)
     matrix = jnp.pad(vertical.reshape(DEVS, LEVELS, DEVS, LEVELS), ((0, 0), (0, PADDED - LEVELS)) * 2).reshape(DEVS * PADDED, DEVS * PADDED)
     packed = call(pack_body, f32(*tiles))(gradient)
     gathered = lax.all_to_all(packed, "lev", 0, 0, tiled=True)
-    scratch = [pltpu.VMEM((DEVS * PADDED, 16 * TILE), jnp.float32)]
-    mixed = call(mix_body, f32(*flat), scratch_shapes=scratch)(matrix, gathered.reshape(flat)).reshape(tiles)
-    mixed = lax.all_to_all(mixed, "lev", 0, 0, tiled=True)
-
-    edge, inner = mixed[:4], mixed[4:]
-    above, below = shifted(edge, "lat", 1, False), shifted(edge, "lat", -1, False)
-    inner_above, inner_below = shifted(inner, "lat", 1, False), shifted(inner, "lat", -1, False)
+    scratch = [pltpu.VMEM((DEVS * PADDED, 8 * TILE), jnp.float32)]
+    halves = []
+    for half in range(2):
+        mixed = call(mix_half(half), f32(flat[0] // 2, TILE), scratch_shapes=scratch)(matrix, gathered.reshape(flat))
+        own = lax.all_to_all(mixed.reshape(DEVS, LEVELS, 8, TILE), "lev", 0, 0, tiled=True)
+        halves.append((own, shifted(own, "lat", 1, False), shifted(own, "lat", -1, False)))
+    early, late = halves
 
     packed = f32(LEVELS, 16, TILE)
-    edge, to_left, to_right = call(edge_body, (f32(LEVELS, ROWS, TILE), packed, packed))(lat, edge, above, below)
+    edge, to_left, to_right = call(edge_body, (f32(LEVELS, ROWS, TILE), packed, packed))(lat, *early)
     from_left, from_right = shifted(to_right, "lon", 1, True), shifted(to_left, "lon", -1, True)
     var_side = f32(LEVELS, 8, TILE)
     to_left, to_right = call(edges_body, (var_side, var_side))(variance)
     var_left, var_right = shifted(to_right, "lon", 1, True), shifted(to_left, "lon", -1, True)
-    inner = call(inner_body, f32(LEVELS, ROWS, 2 * TILE))(lat, inner, inner_above, inner_below)
-
-    back = call(spread_inner_body, f32(LEVELS, ROWS, 2 * TILE))(edge, inner, variance, *inner_matrices())
+    inner = call(inner_body, f32(LEVELS, ROWS, 2 * TILE))(lat, *early, *late)
+
+    back = call(spread_inner_body, f32(LEVELS, ROWS, 2 * TILE))(edge, inner, variance, *bands[:4])
     back_above, back_below = shifted(back, "lat", 1, False), shifted(back, "lat", -1, False)
     sides = (from_left, from_right, variance, var_left, var_right)
-    rim = call(spread_edge_body, f32(LEVELS, ROWS, TILE))(edge, inner, *sides, *edge_matrices())
+    rim = call(spread_edge_body, f32(LEVELS, ROWS, TILE))(edge, inner, *sides, *bands[4:])
     rim_above, rim_below = shifted(rim, "lat", 1, False), shifted(rim, "lat", -1, False)
     back = call(last_inner_body, f32(LEVELS, ROWS, 2 * TILE))(lat, back, back_above, back_below)
     return call(last_edge_body, f32(LEVELS, ROWS, COLS))(lat, rim, rim_above, rim_below, back)

time: 151 us -> 154 us (1.020)
  waiting for transfers between devices: 56.9 us -> 66.7 us
  starting transfers between devices: 78.4 us -> 72.5 us
  other arithmetic: 2.66 us -> 0 us
  Pallas kernels: 10.3 us -> 12.2 us
    ppermute x12, starting transfers between devices: 67.1 us -> 55.3 us  [shifted(): return lax.ppermute(cells, axis, pairs)]
    ppermute x12, waiting for transfers between devices: 33.2 us -> 39.2 us  [shifted(): return lax.ppermute(cells, axis, pairs)]
    all_to_all x1 -> x2, starting transfers between devices: 6.12 us -> 11.9 us  [steps(): lax.all_to_all(mixed.reshape(DEVS, LEVELS, 8, TILE), 'lev', 0, 0, tiled=T...]
    all_to_all x1 -> x2, waiting for transfers between devices: 7.07 us -> 10.8 us  [steps(): lax.all_to_all(mixed.reshape(DEVS, LEVELS, 8, TILE), 'lev', 0, 0, tiled=T...]
    convert_element_type x5 -> x0, other arithmetic: 2.57 us -> none  [split_outside(): return (high.astype(jnp.bfloat16), (values - high).astype(jnp.bfloat16))]
    pallas_call x3 -> x5, Pallas kernels: 2.74 us -> 4.62 us  [the longest x2 2.65 us: steps(): call(mix_half(half), f32(flat[0] // 2, TILE), scratch_shapes=scratch)]
  transfers between devices with their start and end apart: 14 -> 15, of which waited for: 7 -> 10; matrix products, arithmetic and copies ran while one was open for 2% -> 0% of each run, Pallas kernels for 4% -> 3%
where the time goes in v3:
time: 154 us; the launch traced here: 153 us
  starting transfers between devices  72.5 us (47%)
  waiting for transfers between devices  66.7 us (43%)
  Pallas kernels  12.2 us (8%)
  local copies, waits for them, and re-layouts  1.63 us (1%)
    ppermute x12, starting transfers between devices, shifted(): return lax.ppermute(cells, axis, pairs)  55.3 us
    ppermute x12, waiting for transfers between devices, shifted(): return lax.ppermute(cells, axis, pairs)  39.2 us
    all_to_all x1, waiting for transfers between devices, steps(): gathered = lax.all_to_all(packed, 'lev', 0, 0, tiled=True)  16.7 us
    all_to_all x2, starting transfers between devices, steps(): lax.all_to_all(mixed.reshape(DEVS, LEVELS, 8, TILE), 'lev', 0, 0, tiled=T...  11.9 us
    all_to_all x2, waiting for transfers between devices, steps(): lax.all_to_all(mixed.reshape(DEVS, LEVELS, 8, TILE), 'lev', 0, 0, tiled=T...  10.8 us
    all_to_all x1, starting transfers between devices, steps(): gathered = lax.all_to_all(packed, 'lev', 0, 0, tiled=True)  5.23 us
  transfers between devices with their start and end apart: 15, of which 10 were waited for; matrix products, arithmetic and copies ran while one was open for 0% of the time, Pallas kernels for 3%

profile of v3, /device:TPU:94, one launch (start us, length us, event | category | flops | bytes accessed | tf_op | source)
XLA Modules:
  0.0 153.3 jit_solution(2949158193985171131)
XLA Ops:
  0.0 0.0 copy-start.1
  0.0 1.2 copy-done.1
  1.2 1.1 shard_map.38
  2.3 0.0 copy-start.2
  2.3 5.2 %all-to-all-start = ((f32[12,22,8,128]{3,2,1,0:T(8,128)}), f32[12,22,8,128]{3,2,1,0:T(8,128)S(1)}, u32[]{:S(2)}, u32[]{:S(2)}) async-start(f32[12,22,8,128]{3,2,1,0:T(8,128)} %shard_map.38), calls=%async_computation | async-start | bytes 2162688 | tf_op jit(solution)/shard_map/all_to_all | solution.py:238
  7.5 0.0 copy-done.2
  7.5 0.2 reshape.16
  7.8 0.2 reshape.17.matrix
  7.9 16.7 %all-to-all-done = f32[12,22,8,128]{3,2,1,0:T(8,128)S(1)} async-done(((f32[12,22,8,128]{3,2,1,0:T(8,128)}), f32[12,22,8,128]{3,2,1,0:T(8,128)S(1)}, u32[]{:S(2)}, u32[]{:S(2)}) %all-to-all-start) | async-done | bytes 1081376 | tf_op jit(solution)/shard_map/all_to_all | solution.py:238
  24.6 1.3 shard_map.39
  26.0 6.0 %all-to-all-start.1 = ((f32[6,22,8,128]{3,2,1,0:T(8,128)}), f32[6,22,8,128]{3,2,1,0:T(8,128)S(1)}, u32[]{:S(2)}, u32[]{:S(2)}) async-start(f32[6,22,8,128]{3,2,1,0:T(8,128)} %bitcast.1), calls=%async_computation.1 | async-start | bytes 1081344 | tf_op jit(solution)/shard_map/all_to_all | solution.py:243
  31.9 1.3 shard_map.41
  33.2 8.0 %all-to-all-done.1.own.refs_0_ = f32[6,22,8,128]{3,2,1,0:T(8,128)S(1)} async-done(((f32[6,22,8,128]{3,2,1,0:T(8,128)}), f32[6,22,8,128]{3,2,1,0:T(8,128)S(1)}, u32[]{:S(2)}, u32[]{:S(2)}) %all-to-all-start.1) | async-done | bytes 540704 | tf_op jit(solution)/shard_map/all_to_all | solution.py:243
  41.3 6.0 %all-to-all-start.2 = ((f32[6,22,8,128]{3,2,1,0:T(8,128)}), f32[6,22,8,128]{3,2,1,0:T(8,128)S(1)}, u32[]{:S(2)}, u32[]{:S(2)}) async-start(f32[6,22,8,128]{3,2,1,0:T(8,128)} %bitcast.2), calls=%async_computation.2 | async-start | bytes 1081344 | tf_op jit(solution)/shard_map/all_to_all | solution.py:243
  47.2 4.6 %collective-permute-start = (f32[6,22,8,128]{3,2,1,0:T(8,128)S(1)}, f32[6,22,8,128]{3,2,1,0:T(8,128)S(1)}, u32[]{:S(2)}, u32[]{:S(2)}) collective-permute-start(f32[6,22,8,128]{3,2,1,0:T(8,128)S(1)} %all-to-all-done.1.own.refs_0_), channel_id=1, source_target_pairs={{0,24},{24,48},{48,72},{72,96},{96,120},{120,144},{144,168},{168,1... | collective-permute-start | bytes 1622024 | tf_op jit(solution)/shard_map/ppermute | solution.py:228
  51.8 1.9 %collective-permute-start.1 = (f32[6,22,8,128]{3,2,1,0:T(8,128)S(1)}, f32[6,22,8,128]{3,2,1,0:T(8,128)S(1)}, u32[]{:S(2)}, u32[]{:S(2)}) collective-permute-start(f32[6,22,8,128]{3,2,1,0:T(8,128)S(1)} %all-to-all-done.1.own.refs_0_), channel_id=1, source_target_pairs={{24,0},{48,24},{72,48},{96,72},{120,96},{144,120},{168,144},{192,1... | collective-permute-start | bytes 1622024 | tf_op jit(solution)/shard_map/ppermute | solution.py:228
  53.8 2.8 %all-to-all-done.2.refs_3_ = f32[6,22,8,128]{3,2,1,0:T(8,128)S(1)} async-done(((f32[6,22,8,128]{3,2,1,0:T(8,128)}), f32[6,22,8,128]{3,2,1,0:T(8,128)S(1)}, u32[]{:S(2)}, u32[]{:S(2)}) %all-to-all-start.2) | async-done | bytes 540704 | tf_op jit(solution)/shard_map/all_to_all | solution.py:243
  56.6 4.6 %collective-permute-start.2 = (f32[6,22,8,128]{3,2,1,0:T(8,128)S(1)}, f32[6,22,8,128]{3,2,1,0:T(8,128)S(1)}, u32[]{:S(2)}, u32[]{:S(2)}) collective-permute-start(f32[6,22,8,128]{3,2,1,0:T(8,128)S(1)} %all-to-all-done.2.refs_3_), channel_id=1, source_target_pairs={{0,24},{24,48},{48,72},{72,96},{96,120},{120,144},{144,168},{168,1... | collective-permute-start | bytes 1622024 | tf_op jit(solution)/shard_map/ppermute | solution.py:228
  61.2 1.9 %collective-permute-start.3 = (f32[6,22,8,128]{3,2,1,0:T(8,128)S(1)}, f32[6,22,8,128]{3,2,1,0:T(8,128)S(1)}, u32[]{:S(2)}, u32[]{:S(2)}) collective-permute-start(f32[6,22,8,128]{3,2,1,0:T(8,128)S(1)} %all-to-all-done.2.refs_3_), channel_id=1, source_target_pairs={{24,0},{48,24},{72,48},{96,72},{120,96},{144,120},{168,144},{192,1... | collective-permute-start | bytes 1622024 | tf_op jit(solution)/shard_map/ppermute | solution.py:228
  63.1 1.1 shard_map.37
  64.2 0.3 collective-permute-done.above.refs_1_
  64.5 7.7 %collective-permute-done.1.below.refs_2_ = f32[6,22,8,128]{3,2,1,0:T(8,128)S(1)} collective-permute-done((f32[6,22,8,128]{3,2,1,0:T(8,128)S(1)}, f32[6,22,8,128]{3,2,1,0:T(8,128)S(1)}, u32[]{:S(2)}, u32[]{:S(2)}) %collective-permute-start.1) | collective-permute-done | bytes 540704 | tf_op jit(solution)/shard_map/ppermute | solution.py:228
  72.2 0.4 shard_map.40
  72.6 2.6 %collective-permute-done.2.refs_4_ = f32[6,22,8,128]{3,2,1,0:T(8,128)S(1)} collective-permute-done((f32[6,22,8,128]{3,2,1,0:T(8,128)S(1)}, f32[6,22,8,128]{3,2,1,0:T(8,128)S(1)}, u32[]{:S(2)}, u32[]{:S(2)}) %collective-permute-start.2) | collective-permute-done | bytes 540704 | tf_op jit(solution)/shard_map/ppermute | solution.py:228
  75.2 7.4 %collective-permute-done.3.refs_5_ = f32[6,22,8,128]{3,2,1,0:T(8,128)S(1)} collective-permute-done((f32[6,22,8,128]{3,2,1,0:T(8,128)S(1)}, f32[6,22,8,128]{3,2,1,0:T(8,128)S(1)}, u32[]{:S(2)}, u32[]{:S(2)}) %collective-permute-start.3) | collective-permute-done | bytes 540704 | tf_op jit(solution)/shard_map/ppermute | solution.py:228
  82.6 0.5 shard_map.42.inner
  83.2 0.0 copy-done
  83.2 2.8 %shard_map.45.own = f32[22,32,256]{2,1,0:T(8,128)S(1)} custom-call(f32[22,32,128]{2,1,0:T(8,128)S(1)} %get-tuple-element.20.edge, f32[22,32,256]{2,1,0:T(8,128)S(1)} %shard_map.42.inner, f32[22,32,384]{2,1,0:T(8,128)S(1)} %copy-done, bf16[384,384]{1,0:T(8,128)(2,1)S(1)} %get-tuple-element.29.fwd_high, bf16[384,384]{1,0:T(8,128)(2,1)S(1)} %get-tuple-element.30.fwd_low, ...), custom_call_target="tpu_custom_call" | custom-call | tf_op jit(solution)/shard_map/pallas_call | solution.py:255
  85.9 1.9 %collective-permute-start.10 = (f32[22,32,256]{2,1,0:T(8,128)S(1)}, f32[22,32,256]{2,1,0:T(8,128)S(1)}, u32[]{:S(2)}, u32[]{:S(2)}) collective-permute-start(f32[22,32,256]{2,1,0:T(8,128)S(1)} %shard_map.45.own), channel_id=1, source_target_pairs={{0,24},{24,48},{48,72},{72,96},{96,120},{120,144},{144,168},{168,1... | collective-permute-start | bytes 2162696 | tf_op jit(solution)/shard_map/ppermute | solution.py:228
  87.9 3.9 %collective-permute-start.11 = (f32[22,32,256]{2,1,0:T(8,128)S(1)}, f32[22,32,256]{2,1,0:T(8,128)S(1)}, u32[]{:S(2)}, u32[]{:S(2)}) collective-permute-start(f32[22,32,256]{2,1,0:T(8,128)S(1)} %shard_map.45.own), channel_id=1, source_target_pairs={{24,0},{48,24},{72,48},{96,72},{120,96},{144,120},{168,144},{192,1... | collective-permute-start | bytes 2162696 | tf_op jit(solution)/shard_map/ppermute | solution.py:228
  91.8 0.2 shard_map.43
  92.0 12.7 %collective-permute-start.6 = (f32[22,8,128]{2,1,0:T(8,128)S(1)}, f32[22,8,128]{2,1,0:T(8,128)S(1)}, u32[]{:S(2)}, u32[]{:S(2)}) collective-permute-start(f32[22,8,128]{2,1,0:T(8,128)S(1)} %get-tuple-element.23), channel_id=1, source_target_pairs={{0,6},{6,12},{12,18},{18,0},{1,7},{7,13},{13,19},{19,1},{2,8},{8,1... | collective-permute-start | bytes 270344 | tf_op jit(solution)/shard_map/ppermute | solution.py:228
  104.7 5.5 %collective-permute-start.4 = (f32[22,16,128]{2,1,0:T(8,128)S(1)}, f32[22,16,128]{2,1,0:T(8,128)S(1)}, u32[]{:S(2)}, u32[]{:S(2)}) collective-permute-start(f32[22,16,128]{2,1,0:T(8,128)S(1)} %get-tuple-element.21), channel_id=1, source_target_pairs={{0,6},{6,12},{12,18},{18,0},{1,7},{7,13},{13,19},{19,1},{2,8},{8,1... | collective-permute-start | bytes 540680 | tf_op jit(solution)/shard_map/ppermute | solution.py:228
  110.2 3.4 %collective-permute-start.5 = (f32[22,16,128]{2,1,0:T(8,128)S(1)}, f32[22,16,128]{2,1,0:T(8,128)S(1)}, u32[]{:S(2)}, u32[]{:S(2)}) collective-permute-start(f32[22,16,128]{2,1,0:T(8,128)S(1)} %get-tuple-element.22), channel_id=1, source_target_pairs={{0,18},{6,0},{12,6},{18,12},{1,19},{7,1},{13,7},{19,13},{2,20},{8,... | collective-permute-start | bytes 540680 | tf_op jit(solution)/shard_map/ppermute | solution.py:228
  113.6 0.0 collective-permute-done.6.var_left
  113.6 7.0 %collective-permute-start.7 = (f32[22,8,128]{2,1,0:T(8,128)S(1)}, f32[22,8,128]{2,1,0:T(8,128)S(1)}, u32[]{:S(2)}, u32[]{:S(2)}) collective-permute-start(f32[22,8,128]{2,1,0:T(8,128)S(1)} %get-tuple-element.24), channel_id=1, source_target_pairs={{0,18},{6,0},{12,6},{18,12},{1,19},{7,1},{13,7},{19,13},{2,20},{8,... | collective-permute-start | bytes 270344 | tf_op jit(solution)/shard_map/ppermute | solution.py:228
  120.6 11.0 %collective-permute-done.7.var_right = f32[22,8,128]{2,1,0:T(8,128)S(1)} collective-permute-done((f32[22,8,128]{2,1,0:T(8,128)S(1)}, f32[22,8,128]{2,1,0:T(8,128)S(1)}, u32[]{:S(2)}, u32[]{:S(2)}) %collective-permute-start.7) | collective-permute-done | bytes 90144 | tf_op jit(solution)/shard_map/ppermute | solution.py:228
  131.6 0.0 collective-permute-done.4.from_left
  131.6 0.0 collective-permute-done.5.from_right
  131.6 1.8 %shard_map.44.own = f32[22,32,128]{2,1,0:T(8,128)S(1)} custom-call(f32[22,32,128]{2,1,0:T(8,128)S(1)} %get-tuple-element.20.edge, f32[22,32,256]{2,1,0:T(8,128)S(1)} %shard_map.42.inner, f32[22,16,128]{2,1,0:T(8,128)S(1)} %collective-permute-done.4.from_left, f32[22,16,128]{2,1,0:T(8,128)S(1)} %collective-permute-done.5.from_right, ...), custom_call_target="tpu_custom_call" | custom-call | tf_op jit(solution)/shard_map/pallas_call | solution.py:258
  133.4 5.9 %collective-permute-start.8 = (f32[22,32,128]{2,1,0:T(8,128)S(1)}, f32[22,32,128]{2,1,0:T(8,128)S(1)}, u32[]{:S(2)}, u32[]{:S(2)}) collective-permute-start(f32[22,32,128]{2,1,0:T(8,128)S(1)} %shard_map.44.own), channel_id=1, source_target_pairs={{0,24},{24,48},{48,72},{72,96},{96,120},{120,144},{144,168},{168,1... | collective-permute-start | bytes 1081352 | tf_op jit(solution)/shard_map/ppermute | solution.py:228
  139.3 1.9 %collective-permute-start.9 = (f32[22,32,128]{2,1,0:T(8,128)S(1)}, f32[22,32,128]{2,1,0:T(8,128)S(1)}, u32[]{:S(2)}, u32[]{:S(2)}) collective-permute-start(f32[22,32,128]{2,1,0:T(8,128)S(1)} %shard_map.44.own), channel_id=1, source_target_pairs={{24,0},{48,24},{72,48},{96,72},{120,96},{144,120},{168,144},{192,1... | collective-permute-start | bytes 1081352 | tf_op jit(solution)/shard_map/ppermute | solution.py:228
  141.2 0.0 collective-permute-done.10.above
  141.2 0.0 collective-permute-done.11.below
  141.2 0.5 shard_map.46.inner
  141.8 2.5 %collective-permute-done.8.above = f32[22,32,128]{2,1,0:T(8,128)S(1)} collective-permute-done((f32[22,32,128]{2,1,0:T(8,128)S(1)}, f32[22,32,128]{2,1,0:T(8,128)S(1)}, u32[]{:S(2)}, u32[]{:S(2)}) %collective-permute-start.8) | collective-permute-done | bytes 360480 | tf_op jit(solution)/shard_map/ppermute | solution.py:228
  144.2 7.7 %collective-permute-done.9.below = f32[22,32,128]{2,1,0:T(8,128)S(1)} collective-permute-done((f32[22,32,128]{2,1,0:T(8,128)S(1)}, f32[22,32,128]{2,1,0:T(8,128)S(1)}, u32[]{:S(2)}, u32[]{:S(2)}) %collective-permute-start.9) | collective-permute-done | bytes 360480 | tf_op jit(solution)/shard_map/ppermute | solution.py:228
  151.9 1.3 shard_map.47
  (2 shorter events, 0.1 us)
Async XLA Ops:
  0.0 1.2 copy-start.1
  2.3 5.2 %copy-start.2 = (f32[132,132]{1,0:T(8,128)S(1)}, f32[132,132]{1,0:T(8,128)}, u32[]{:S(2)}) copy-start(f32[132,132]{1,0:T(8,128)} %param.4) | copy-start | bytes 209092
  2.3 22.3 %all-to-all-start = ((f32[12,22,8,128]{3,2,1,0:T(8,128)}), f32[12,22,8,128]{3,2,1,0:T(8,128)S(1)}, u32[]{:S(2)}, u32[]{:S(2)}) async-start(f32[12,22,8,128]{3,2,1,0:T(8,128)} %shard_map.38), calls=%async_computation | async-start | bytes 2162688 | tf_op jit(solution)/shard_map/all_to_all | solution.py:238
  26.0 15.3 %all-to-all-start.1 = ((f32[6,22,8,128]{3,2,1,0:T(8,128)}), f32[6,22,8,128]{3,2,1,0:T(8,128)S(1)}, u32[]{:S(2)}, u32[]{:S(2)}) async-start(f32[6,22,8,128]{3,2,1,0:T(8,128)} %bitcast.1), calls=%async_computation.1 | async-start | bytes 1081344 | tf_op jit(solution)/shard_map/all_to_all | solution.py:243
  41.3 15.3 %all-to-all-start.2 = ((f32[6,22,8,128]{3,2,1,0:T(8,128)}), f32[6,22,8,128]{3,2,1,0:T(8,128)S(1)}, u32[]{:S(2)}, u32[]{:S(2)}) async-start(f32[6,22,8,128]{3,2,1,0:T(8,128)} %bitcast.2), calls=%async_computation.2 | async-start | bytes 1081344 | tf_op jit(solution)/shard_map/all_to_all | solution.py:243
  47.2 17.3 %collective-permute-start = (f32[6,22,8,128]{3,2,1,0:T(8,128)S(1)}, f32[6,22,8,128]{3,2,1,0:T(8,128)S(1)}, u32[]{:S(2)}, u32[]{:S(2)}) collective-permute-start(f32[6,22,8,128]{3,2,1,0:T(8,128)S(1)} %all-to-all-done.1.own.refs_0_), channel_id=1, source_target_pairs={{0,24},{24,48},{48,72},{72,96},{96,120},{120,144},{144,168},{168,1... | collective-permute-start | bytes 1622024 | tf_op jit(solution)/shard_map/ppermute | solution.py:228
  51.8 20.4 %collective-permute-start.1 = (f32[6,22,8,128]{3,2,1,0:T(8,128)S(1)}, f32[6,22,8,128]{3,2,1,0:T(8,128)S(1)}, u32[]{:S(2)}, u32[]{:S(2)}) collective-permute-start(f32[6,22,8,128]{3,2,1,0:T(8,128)S(1)} %all-to-all-done.1.own.refs_0_), channel_id=1, source_target_pairs={{24,0},{48,24},{72,48},{96,72},{120,96},{144,120},{168,144},{192,1... | collective-permute-start | bytes 1622024 | tf_op jit(solution)/shard_map/ppermute | solution.py:228
  56.6 18.7 %collective-permute-start.2 = (f32[6,22,8,128]{3,2,1,0:T(8,128)S(1)}, f32[6,22,8,128]{3,2,1,0:T(8,128)S(1)}, u32[]{:S(2)}, u32[]{:S(2)}) collective-permute-start(f32[6,22,8,128]{3,2,1,0:T(8,128)S(1)} %all-to-all-done.2.refs_3_), channel_id=1, source_target_pairs={{0,24},{24,48},{48,72},{72,96},{96,120},{120,144},{144,168},{168,1... | collective-permute-start | bytes 1622024 | tf_op jit(solution)/shard_map/ppermute | solution.py:228
  61.2 21.5 %collective-permute-start.3 = (f32[6,22,8,128]{3,2,1,0:T(8,128)S(1)}, f32[6,22,8,128]{3,2,1,0:T(8,128)S(1)}, u32[]{:S(2)}, u32[]{:S(2)}) collective-permute-start(f32[6,22,8,128]{3,2,1,0:T(8,128)S(1)} %all-to-all-done.2.refs_3_), channel_id=1, source_target_pairs={{24,0},{48,24},{72,48},{96,72},{120,96},{144,120},{168,144},{192,1... | collective-permute-start | bytes 1622024 | tf_op jit(solution)/shard_map/ppermute | solution.py:228
  72.6 10.6 %copy-start = (f32[22,32,384]{2,1,0:T(8,128)S(1)}, f32[22,32,384]{2,1,0:T(8,128)}, u32[]{:S(2)}) copy-start(f32[22,32,384]{2,1,0:T(8,128)} %variance.3) | copy-start | bytes 3244036
  85.9 55.3 %collective-permute-start.10 = (f32[22,32,256]{2,1,0:T(8,128)S(1)}, f32[22,32,256]{2,1,0:T(8,128)S(1)}, u32[]{:S(2)}, u32[]{:S(2)}) collective-permute-start(f32[22,32,256]{2,1,0:T(8,128)S(1)} %shard_map.45.own), channel_id=1, source_target_pairs={{0,24},{24,48},{48,72},{72,96},{96,120},{120,144},{144,168},{168,1... | collective-permute-start | bytes 2162696 | tf_op jit(solution)/shard_map/ppermute | solution.py:228
  87.9 53.4 %collective-permute-start.11 = (f32[22,32,256]{2,1,0:T(8,128)S(1)}, f32[22,32,256]{2,1,0:T(8,128)S(1)}, u32[]{:S(2)}, u32[]{:S(2)}) collective-permute-start(f32[22,32,256]{2,1,0:T(8,128)S(1)} %shard_map.45.own), channel_id=1, source_target_pairs={{24,0},{48,24},{72,48},{96,72},{120,96},{144,120},{168,144},{192,1... | collective-permute-start | bytes 2162696 | tf_op jit(solution)/shard_map/ppermute | solution.py:228
  92.0 21.6 %collective-permute-start.6 = (f32[22,8,128]{2,1,0:T(8,128)S(1)}, f32[22,8,128]{2,1,0:T(8,128)S(1)}, u32[]{:S(2)}, u32[]{:S(2)}) collective-permute-start(f32[22,8,128]{2,1,0:T(8,128)S(1)} %get-tuple-element.23), channel_id=1, source_target_pairs={{0,6},{6,12},{12,18},{18,0},{1,7},{7,13},{13,19},{19,1},{2,8},{8,1... | collective-permute-start | bytes 270344 | tf_op jit(solution)/shard_map/ppermute | solution.py:228
  104.7 26.9 %collective-permute-start.4 = (f32[22,16,128]{2,1,0:T(8,128)S(1)}, f32[22,16,128]{2,1,0:T(8,128)S(1)}, u32[]{:S(2)}, u32[]{:S(2)}) collective-permute-start(f32[22,16,128]{2,1,0:T(8,128)S(1)} %get-tuple-element.21), channel_id=1, source_target_pairs={{0,6},{6,12},{12,18},{18,0},{1,7},{7,13},{13,19},{19,1},{2,8},{8,1... | collective-permute-start | bytes 540680 | tf_op jit(solution)/shard_map/ppermute | solution.py:228
  110.2 21.4 %collective-permute-start.5 = (f32[22,16,128]{2,1,0:T(8,128)S(1)}, f32[22,16,128]{2,1,0:T(8,128)S(1)}, u32[]{:S(2)}, u32[]{:S(2)}) collective-permute-start(f32[22,16,128]{2,1,0:T(8,128)S(1)} %get-tuple-element.22), channel_id=1, source_target_pairs={{0,18},{6,0},{12,6},{18,12},{1,19},{7,1},{13,7},{19,13},{2,20},{8,... | collective-permute-start | bytes 540680 | tf_op jit(solution)/shard_map/ppermute | solution.py:228
  113.6 18.0 %collective-permute-start.7 = (f32[22,8,128]{2,1,0:T(8,128)S(1)}, f32[22,8,128]{2,1,0:T(8,128)S(1)}, u32[]{:S(2)}, u32[]{:S(2)}) collective-permute-start(f32[22,8,128]{2,1,0:T(8,128)S(1)} %get-tuple-element.24), channel_id=1, source_target_pairs={{0,18},{6,0},{12,6},{18,12},{1,19},{7,1},{13,7},{19,13},{2,20},{8,... | collective-permute-start | bytes 270344 | tf_op jit(solution)/shard_map/ppermute | solution.py:228
  133.4 10.8 %collective-permute-start.8 = (f32[22,32,128]{2,1,0:T(8,128)S(1)}, f32[22,32,128]{2,1,0:T(8,128)S(1)}, u32[]{:S(2)}, u32[]{:S(2)}) collective-permute-start(f32[22,32,128]{2,1,0:T(8,128)S(1)} %shard_map.44.own), channel_id=1, source_target_pairs={{0,24},{24,48},{48,72},{72,96},{96,120},{120,144},{144,168},{168,1... | collective-permute-start | bytes 1081352 | tf_op jit(solution)/shard_map/ppermute | solution.py:228
  139.3 12.6 %collective-permute-start.9 = (f32[22,32,128]{2,1,0:T(8,128)S(1)}, f32[22,32,128]{2,1,0:T(8,128)S(1)}, u32[]{:S(2)}, u32[]{:S(2)}) collective-permute-start(f32[22,32,128]{2,1,0:T(8,128)S(1)} %shard_map.44.own), channel_id=1, source_target_pairs={{24,0},{48,24},{72,48},{96,72},{120,96},{144,120},{168,144},{192,1... | collective-permute-start | bytes 1081352 | tf_op jit(solution)/shard_map/ppermute | solution.py:228

commit v4 on v3

--- a/solution.py
+++ b/solution.py
@@ -14,6 +14,8 @@
 DEVS = 6
 PADDED = 24
 TILE = 128
+CUTS = 2
+PART = LEVELS // CUTS
 
 
 def tap_scale():
@@ -172,11 +174,11 @@
 
 
 def spread_inner_body(edge, inner, variance, fwd_high, fwd_low, adj_high, adj_low, out):
-    count = LEVELS * ROWS
+    count = PART * ROWS
     held = jnp.concatenate([edge[...].reshape(count, TILE), inner[...].reshape(count, 2 * TILE)], axis=1)
     smooth = exact_right(held, fwd_high[...], fwd_low[...])
     scaled = smooth * variance[...].reshape(count, COLS)
-    out[...] = exact_right(scaled, adj_high[...], adj_low[...]).reshape(LEVELS, ROWS, 2 * TILE)
+    out[...] = exact_right(scaled, adj_high[...], adj_low[...]).reshape(PART, ROWS, 2 * TILE)
 
 
 def spread_edge_body(edge, inner, from_left, from_right, variance, var_left, var_right, fwd_high, fwd_low, adj_high, adj_low, out):
@@ -202,10 +204,13 @@
     out[...] = exact_right(scaled, adj_high[...], adj_low[...]).reshape(LEVELS, ROWS, TILE)
 
 
-def last_inner_body(matrix, own, above, below, out):
-    stacked = matrix[...]
-    for level in range(LEVELS):
-        out[level] = exact_left(stacked, jnp.concatenate([above[level], own[level], below[level]], axis=0))
+def last_inner_body(matrix, *refs):
+    stacked, out = matrix[...], refs[-1]
+    for cut in range(CUTS):
+        own, above, below = refs[3 * cut : 3 * cut + 3]
+        for level in range(PART):
+            cells = jnp.concatenate([above[level], own[level], below[level]], axis=0)
+            out[PART * cut + level] = exact_left(stacked, cells)
 
 
 def last_edge_body(matrix, own, above, below, inner, out):
@@ -252,12 +257,21 @@
     var_left, var_right = shifted(to_right, "lon", 1, True), shifted(to_left, "lon", -1, True)
     inner = call(inner_body, f32(LEVELS, ROWS, 2 * TILE))(lat, *early, *late)
 
-    back = call(spread_inner_body, f32(LEVELS, ROWS, 2 * TILE))(edge, inner, variance, *bands[:4])
-    back_above, back_below = shifted(back, "lat", 1, False), shifted(back, "lat", -1, False)
+    backs = []
+    for cut in range(CUTS):
+
+        def block(array, cut=cut):
+            return pl.BlockSpec((PART,) + array.shape[1:], lambda i: (cut, 0, 0))
+
+        arrays = (edge, inner, variance)
+        specs = [block(array) for array in arrays] + [pl.BlockSpec(m.shape, lambda i: (0, 0)) for m in bands[:4]]
+        shape = (PART, ROWS, 2 * TILE)
+        own = call(spread_inner_body, f32(*shape), grid=(1,), in_specs=specs, out_specs=pl.BlockSpec(shape, lambda i: (0, 0, 0)))(*arrays, *bands[:4])
+        backs += [own, shifted(own, "lat", 1, False), shifted(own, "lat", -1, False)]
     sides = (from_left, from_right, variance, var_left, var_right)
     rim = call(spread_edge_body, f32(LEVELS, ROWS, TILE))(edge, inner, *sides, *bands[4:])
     rim_above, rim_below = shifted(rim, "lat", 1, False), shifted(rim, "lat", -1, False)
-    back = call(last_inner_body, f32(LEVELS, ROWS, 2 * TILE))(lat, back, back_above, back_below)
+    back = call(last_inner_body, f32(LEVELS, ROWS, 2 * TILE))(lat, *backs)
     return call(last_edge_body, f32(LEVELS, ROWS, COLS))(lat, rim, rim_above, rim_below, back)
 
 

time: 154 us -> 152 us (0.987)
  the two profiles are of different devices: /device:TPU:94 before, /device:TPU:158 now
where the time goes in v4:
time: 152 us
  starting transfers between devices  71.6 us (47%)
  waiting for transfers between devices  65.6 us (43%)
  Pallas kernels  12.4 us (8%)
  local copies, waits for them, and re-layouts  1.63 us (1%)
    ppermute x14, starting transfers between devices, shifted(): return lax.ppermute(cells, axis, pairs)  55.2 us
    ppermute x14, waiting for transfers between devices, shifted(): return lax.ppermute(cells, axis, pairs)  38.3 us
    all_to_all x1, waiting for transfers between devices, steps(): gathered = lax.all_to_all(packed, 'lev', 0, 0, tiled=True)  16.6 us
    all_to_all x2, starting transfers between devices, steps(): lax.all_to_all(mixed.reshape(DEVS, LEVELS, 8, TILE), 'lev', 0, 0, tiled=T...  12.1 us
    all_to_all x2, waiting for transfers between devices, steps(): lax.all_to_all(mixed.reshape(DEVS, LEVELS, 8, TILE), 'lev', 0, 0, tiled=T...  10.7 us
    all_to_all x1, starting transfers between devices, steps(): gathered = lax.all_to_all(packed, 'lev', 0, 0, tiled=True)  4.33 us
  transfers between devices with their start and end apart: 17, of which 12 were waited for; matrix products, arithmetic and copies ran while one was open for 0% of the time, Pallas kernels for 4%

profile of v4, /device:TPU:158, one launch (start us, length us, event | category | flops | bytes accessed | tf_op | source)
XLA Modules:
  0.0 151.5 jit_solution(1382453713750313790)
XLA Ops:
  0.0 1.2 copy-done.1
  1.2 1.1 shard_map.38
  2.3 4.3 %all-to-all-start = ((f32[12,22,8,128]{3,2,1,0:T(8,128)}), f32[12,22,8,128]{3,2,1,0:T(8,128)S(1)}, u32[]{:S(2)}, u32[]{:S(2)}) async-start(f32[12,22,8,128]{3,2,1,0:T(8,128)} %shard_map.38), calls=%async_computation | async-start | bytes 2162688 | tf_op jit(solution)/shard_map/all_to_all | solution.py:243
  6.6 0.2 reshape.16
  6.9 0.2 reshape.17.matrix
  7.0 16.6 %all-to-all-done = f32[12,22,8,128]{3,2,1,0:T(8,128)S(1)} async-done(((f32[12,22,8,128]{3,2,1,0:T(8,128)}), f32[12,22,8,128]{3,2,1,0:T(8,128)S(1)}, u32[]{:S(2)}, u32[]{:S(2)}) %all-to-all-start) | async-done | bytes 1081376 | tf_op jit(solution)/shard_map/all_to_all | solution.py:243
  23.6 1.3 shard_map.39
  25.0 6.1 %all-to-all-start.1 = ((f32[6,22,8,128]{3,2,1,0:T(8,128)}), f32[6,22,8,128]{3,2,1,0:T(8,128)S(1)}, u32[]{:S(2)}, u32[]{:S(2)}) async-start(f32[6,22,8,128]{3,2,1,0:T(8,128)} %bitcast.1), calls=%async_computation.1 | async-start | bytes 1081344 | tf_op jit(solution)/shard_map/all_to_all | solution.py:248
  31.0 1.3 shard_map.41
  32.3 8.0 %all-to-all-done.1.own.refs_0_ = f32[6,22,8,128]{3,2,1,0:T(8,128)S(1)} async-done(((f32[6,22,8,128]{3,2,1,0:T(8,128)}), f32[6,22,8,128]{3,2,1,0:T(8,128)S(1)}, u32[]{:S(2)}, u32[]{:S(2)}) %all-to-all-start.1) | async-done | bytes 540704 | tf_op jit(solution)/shard_map/all_to_all | solution.py:248
  40.3 6.0 %all-to-all-start.2 = ((f32[6,22,8,128]{3,2,1,0:T(8,128)}), f32[6,22,8,128]{3,2,1,0:T(8,128)S(1)}, u32[]{:S(2)}, u32[]{:S(2)}) async-start(f32[6,22,8,128]{3,2,1,0:T(8,128)} %bitcast.2), calls=%async_computation.2 | async-start | bytes 1081344 | tf_op jit(solution)/shard_map/all_to_all | solution.py:248
  46.3 4.6 %collective-permute-start = (f32[6,22,8,128]{3,2,1,0:T(8,128)S(1)}, f32[6,22,8,128]{3,2,1,0:T(8,128)S(1)}, u32[]{:S(2)}, u32[]{:S(2)}) collective-permute-start(f32[6,22,8,128]{3,2,1,0:T(8,128)S(1)} %all-to-all-done.1.own.refs_0_), channel_id=1, source_target_pairs={{0,24},{24,48},{48,72},{72,96},{96,120},{120,144},{144,168},{168,1... | collective-permute-start | bytes 1622024 | tf_op jit(solution)/shard_map/ppermute | solution.py:233
  50.9 1.9 %collective-permute-start.1 = (f32[6,22,8,128]{3,2,1,0:T(8,128)S(1)}, f32[6,22,8,128]{3,2,1,0:T(8,128)S(1)}, u32[]{:S(2)}, u32[]{:S(2)}) collective-permute-start(f32[6,22,8,128]{3,2,1,0:T(8,128)S(1)} %all-to-all-done.1.own.refs_0_), channel_id=1, source_target_pairs={{24,0},{48,24},{72,48},{96,72},{120,96},{144,120},{168,144},{192,1... | collective-permute-start | bytes 1622024 | tf_op jit(solution)/shard_map/ppermute | solution.py:233
  52.9 2.7 %all-to-all-done.2.refs_3_ = f32[6,22,8,128]{3,2,1,0:T(8,128)S(1)} async-done(((f32[6,22,8,128]{3,2,1,0:T(8,128)}), f32[6,22,8,128]{3,2,1,0:T(8,128)S(1)}, u32[]{:S(2)}, u32[]{:S(2)}) %all-to-all-start.2) | async-done | bytes 540704 | tf_op jit(solution)/shard_map/all_to_all | solution.py:248
  55.6 4.6 %collective-permute-start.2 = (f32[6,22,8,128]{3,2,1,0:T(8,128)S(1)}, f32[6,22,8,128]{3,2,1,0:T(8,128)S(1)}, u32[]{:S(2)}, u32[]{:S(2)}) collective-permute-start(f32[6,22,8,128]{3,2,1,0:T(8,128)S(1)} %all-to-all-done.2.refs_3_), channel_id=1, source_target_pairs={{0,24},{24,48},{48,72},{72,96},{96,120},{120,144},{144,168},{168,1... | collective-permute-start | bytes 1622024 | tf_op jit(solution)/shard_map/ppermute | solution.py:233
  60.2 1.9 %collective-permute-start.3 = (f32[6,22,8,128]{3,2,1,0:T(8,128)S(1)}, f32[6,22,8,128]{3,2,1,0:T(8,128)S(1)}, u32[]{:S(2)}, u32[]{:S(2)}) collective-permute-start(f32[6,22,8,128]{3,2,1,0:T(8,128)S(1)} %all-to-all-done.2.refs_3_), channel_id=1, source_target_pairs={{24,0},{48,24},{72,48},{96,72},{120,96},{144,120},{168,144},{192,1... | collective-permute-start | bytes 1622024 | tf_op jit(solution)/shard_map/ppermute | solution.py:233
  62.1 1.1 shard_map.37
  63.2 0.4 collective-permute-done.above.refs_1_
  63.6 7.7 %collective-permute-done.1.below.refs_2_ = f32[6,22,8,128]{3,2,1,0:T(8,128)S(1)} collective-permute-done((f32[6,22,8,128]{3,2,1,0:T(8,128)S(1)}, f32[6,22,8,128]{3,2,1,0:T(8,128)S(1)}, u32[]{:S(2)}, u32[]{:S(2)}) %collective-permute-start.1) | collective-permute-done | bytes 540704 | tf_op jit(solution)/shard_map/ppermute | solution.py:233
  71.3 0.4 shard_map.40
  71.7 2.6 %collective-permute-done.2.refs_4_ = f32[6,22,8,128]{3,2,1,0:T(8,128)S(1)} collective-permute-done((f32[6,22,8,128]{3,2,1,0:T(8,128)S(1)}, f32[6,22,8,128]{3,2,1,0:T(8,128)S(1)}, u32[]{:S(2)}, u32[]{:S(2)}) %collective-permute-start.2) | collective-permute-done | bytes 540704 | tf_op jit(solution)/shard_map/ppermute | solution.py:233
  74.3 7.4 %collective-permute-done.3.refs_5_ = f32[6,22,8,128]{3,2,1,0:T(8,128)S(1)} collective-permute-done((f32[6,22,8,128]{3,2,1,0:T(8,128)S(1)}, f32[6,22,8,128]{3,2,1,0:T(8,128)S(1)}, u32[]{:S(2)}, u32[]{:S(2)}) %collective-permute-start.3) | collective-permute-done | bytes 540704 | tf_op jit(solution)/shard_map/ppermute | solution.py:233
  81.7 0.5 shard_map.42.inner
  82.3 1.5 shard_map.46.refs_3_
  83.8 1.9 %collective-permute-start.12 = (f32[11,32,256]{2,1,0:T(8,128)S(1)}, f32[11,32,256]{2,1,0:T(8,128)S(1)}, u32[]{:S(2)}, u32[]{:S(2)}) collective-permute-start(f32[11,32,256]{2,1,0:T(8,128)S(1)} %shard_map.46.refs_3_), channel_id=1, source_target_pairs={{0,24},{24,48},{48,72},{72,96},{96,120},{120,144},{144,168},{168,1... | collective-permute-start | bytes 1081352 | tf_op jit(solution)/shard_map/ppermute | solution.py:233
  85.7 12.7 %collective-permute-start.4 = (f32[22,16,128]{2,1,0:T(8,128)S(1)}, f32[22,16,128]{2,1,0:T(8,128)S(1)}, u32[]{:S(2)}, u32[]{:S(2)}) collective-permute-start(f32[22,16,128]{2,1,0:T(8,128)S(1)} %get-tuple-element.21), channel_id=1, source_target_pairs={{0,6},{6,12},{12,18},{18,0},{1,7},{7,13},{13,19},{19,1},{2,8},{8,1... | collective-permute-start | bytes 540680 | tf_op jit(solution)/shard_map/ppermute | solution.py:233
  98.4 1.9 %collective-permute-start.5 = (f32[22,16,128]{2,1,0:T(8,128)S(1)}, f32[22,16,128]{2,1,0:T(8,128)S(1)}, u32[]{:S(2)}, u32[]{:S(2)}) collective-permute-start(f32[22,16,128]{2,1,0:T(8,128)S(1)} %get-tuple-element.22), channel_id=1, source_target_pairs={{0,18},{6,0},{12,6},{18,12},{1,19},{7,1},{13,7},{19,13},{2,20},{8,... | collective-permute-start | bytes 540680 | tf_op jit(solution)/shard_map/ppermute | solution.py:233
  100.4 0.2 shard_map.43
  100.6 6.9 %collective-permute-start.6 = (f32[22,8,128]{2,1,0:T(8,128)S(1)}, f32[22,8,128]{2,1,0:T(8,128)S(1)}, u32[]{:S(2)}, u32[]{:S(2)}) collective-permute-start(f32[22,8,128]{2,1,0:T(8,128)S(1)} %get-tuple-element.23), channel_id=1, source_target_pairs={{0,6},{6,12},{12,18},{18,0},{1,7},{7,13},{13,19},{19,1},{2,8},{8,1... | collective-permute-start | bytes 270344 | tf_op jit(solution)/shard_map/ppermute | solution.py:233
  107.5 1.9 %collective-permute-start.7 = (f32[22,8,128]{2,1,0:T(8,128)S(1)}, f32[22,8,128]{2,1,0:T(8,128)S(1)}, u32[]{:S(2)}, u32[]{:S(2)}) collective-permute-start(f32[22,8,128]{2,1,0:T(8,128)S(1)} %get-tuple-element.24), channel_id=1, source_target_pairs={{0,18},{6,0},{12,6},{18,12},{1,19},{7,1},{13,7},{19,13},{2,20},{8,... | collective-permute-start | bytes 270344 | tf_op jit(solution)/shard_map/ppermute | solution.py:233
  109.5 1.5 shard_map.45.refs_0_
  111.0 4.7 %collective-permute-done.6.var_left = f32[22,8,128]{2,1,0:T(8,128)S(1)} collective-permute-done((f32[22,8,128]{2,1,0:T(8,128)S(1)}, f32[22,8,128]{2,1,0:T(8,128)S(1)}, u32[]{:S(2)}, u32[]{:S(2)}) %collective-permute-start.6) | collective-permute-done | bytes 90144 | tf_op jit(solution)/shard_map/ppermute | solution.py:233
  115.6 2.9 %collective-permute-start.13 = (f32[11,32,256]{2,1,0:T(8,128)S(1)}, f32[11,32,256]{2,1,0:T(8,128)S(1)}, u32[]{:S(2)}, u32[]{:S(2)}) collective-permute-start(f32[11,32,256]{2,1,0:T(8,128)S(1)} %shard_map.46.refs_3_), channel_id=1, source_target_pairs={{24,0},{48,24},{72,48},{96,72},{120,96},{144,120},{168,144},{192,1... | collective-permute-start | bytes 1081352 | tf_op jit(solution)/shard_map/ppermute | solution.py:233
  118.5 3.5 %collective-permute-done.7.var_right = f32[22,8,128]{2,1,0:T(8,128)S(1)} collective-permute-done((f32[22,8,128]{2,1,0:T(8,128)S(1)}, f32[22,8,128]{2,1,0:T(8,128)S(1)}, u32[]{:S(2)}, u32[]{:S(2)}) %collective-permute-start.7) | collective-permute-done | bytes 90144 | tf_op jit(solution)/shard_map/ppermute | solution.py:233
  122.1 2.7 %collective-permute-start.10 = (f32[11,32,256]{2,1,0:T(8,128)S(1)}, f32[11,32,256]{2,1,0:T(8,128)S(1)}, u32[]{:S(2)}, u32[]{:S(2)}) collective-permute-start(f32[11,32,256]{2,1,0:T(8,128)S(1)} %shard_map.45.refs_0_), channel_id=1, source_target_pairs={{0,24},{24,48},{48,72},{72,96},{96,120},{120,144},{144,168},{168,1... | collective-permute-start | bytes 1081352 | tf_op jit(solution)/shard_map/ppermute | solution.py:233
  124.8 0.0 collective-permute-done.4.from_left
  124.8 3.1 %collective-permute-start.11 = (f32[11,32,256]{2,1,0:T(8,128)S(1)}, f32[11,32,256]{2,1,0:T(8,128)S(1)}, u32[]{:S(2)}, u32[]{:S(2)}) collective-permute-start(f32[11,32,256]{2,1,0:T(8,128)S(1)} %shard_map.45.refs_0_), channel_id=1, source_target_pairs={{24,0},{48,24},{72,48},{96,72},{120,96},{144,120},{168,144},{192,1... | collective-permute-start | bytes 1081352 | tf_op jit(solution)/shard_map/ppermute | solution.py:233
  127.9 0.0 collective-permute-done.5.from_right
  127.9 1.7 %shard_map.44.own = f32[22,32,128]{2,1,0:T(8,128)S(1)} custom-call(f32[22,32,128]{2,1,0:T(8,128)S(1)} %get-tuple-element.20.edge, f32[22,32,256]{2,1,0:T(8,128)S(1)} %shard_map.42.inner, f32[22,16,128]{2,1,0:T(8,128)S(1)} %collective-permute-done.4.from_left, f32[22,16,128]{2,1,0:T(8,128)S(1)} %collective-permute-done.5.from_right, ...), custom_call_target="tpu_custom_call" | custom-call | tf_op jit(solution)/shard_map/pallas_call | solution.py:272
  129.7 6.1 %collective-permute-start.8 = (f32[22,32,128]{2,1,0:T(8,128)S(1)}, f32[22,32,128]{2,1,0:T(8,128)S(1)}, u32[]{:S(2)}, u32[]{:S(2)}) collective-permute-start(f32[22,32,128]{2,1,0:T(8,128)S(1)} %shard_map.44.own), channel_id=1, source_target_pairs={{0,24},{24,48},{48,72},{72,96},{96,120},{120,144},{144,168},{168,1... | collective-permute-start | bytes 1081352 | tf_op jit(solution)/shard_map/ppermute | solution.py:233
  135.8 0.0 collective-permute-done.12.refs_4_
  135.8 1.9 %collective-permute-start.9 = (f32[22,32,128]{2,1,0:T(8,128)S(1)}, f32[22,32,128]{2,1,0:T(8,128)S(1)}, u32[]{:S(2)}, u32[]{:S(2)}) collective-permute-start(f32[22,32,128]{2,1,0:T(8,128)S(1)} %shard_map.44.own), channel_id=1, source_target_pairs={{24,0},{48,24},{72,48},{96,72},{120,96},{144,120},{168,144},{192,1... | collective-permute-start | bytes 1081352 | tf_op jit(solution)/shard_map/ppermute | solution.py:233
  137.7 0.0 collective-permute-done.10.refs_1_
  137.7 2.1 %collective-permute-done.11.refs_2_ = f32[11,32,256]{2,1,0:T(8,128)S(1)} collective-permute-done((f32[11,32,256]{2,1,0:T(8,128)S(1)}, f32[11,32,256]{2,1,0:T(8,128)S(1)}, u32[]{:S(2)}, u32[]{:S(2)}) %collective-permute-start.11) | collective-permute-done | bytes 360480 | tf_op jit(solution)/shard_map/ppermute | solution.py:233
  139.8 0.5 shard_map.47.inner
  140.3 2.4 %collective-permute-done.8.above = f32[22,32,128]{2,1,0:T(8,128)S(1)} collective-permute-done((f32[22,32,128]{2,1,0:T(8,128)S(1)}, f32[22,32,128]{2,1,0:T(8,128)S(1)}, u32[]{:S(2)}, u32[]{:S(2)}) %collective-permute-start.8) | collective-permute-done | bytes 360480 | tf_op jit(solution)/shard_map/ppermute | solution.py:233
  142.8 7.4 %collective-permute-done.9.below = f32[22,32,128]{2,1,0:T(8,128)S(1)} collective-permute-done((f32[22,32,128]{2,1,0:T(8,128)S(1)}, f32[22,32,128]{2,1,0:T(8,128)S(1)}, u32[]{:S(2)}, u32[]{:S(2)}) %collective-permute-start.9) | collective-permute-done | bytes 360480 | tf_op jit(solution)/shard_map/ppermute | solution.py:233
  150.2 1.3 shard_map.48
  (7 shorter events, 0.1 us)
Async XLA Ops:
  0.0 1.2 copy-start.1
  2.3 4.3 %copy-start.2 = (f32[132,132]{1,0:T(8,128)S(1)}, f32[132,132]{1,0:T(8,128)}, u32[]{:S(2)}) copy-start(f32[132,132]{1,0:T(8,128)} %param.4) | copy-start | bytes 209092
  2.3 21.3 %all-to-all-start = ((f32[12,22,8,128]{3,2,1,0:T(8,128)}), f32[12,22,8,128]{3,2,1,0:T(8,128)S(1)}, u32[]{:S(2)}, u32[]{:S(2)}) async-start(f32[12,22,8,128]{3,2,1,0:T(8,128)} %shard_map.38), calls=%async_computation | async-start | bytes 2162688 | tf_op jit(solution)/shard_map/all_to_all | solution.py:243
  25.0 15.3 %all-to-all-start.1 = ((f32[6,22,8,128]{3,2,1,0:T(8,128)}), f32[6,22,8,128]{3,2,1,0:T(8,128)S(1)}, u32[]{:S(2)}, u32[]{:S(2)}) async-start(f32[6,22,8,128]{3,2,1,0:T(8,128)} %bitcast.1), calls=%async_computation.1 | async-start | bytes 1081344 | tf_op jit(solution)/shard_map/all_to_all | solution.py:248
  40.3 15.3 %all-to-all-start.2 = ((f32[6,22,8,128]{3,2,1,0:T(8,128)}), f32[6,22,8,128]{3,2,1,0:T(8,128)S(1)}, u32[]{:S(2)}, u32[]{:S(2)}) async-start(f32[6,22,8,128]{3,2,1,0:T(8,128)} %bitcast.2), calls=%async_computation.2 | async-start | bytes 1081344 | tf_op jit(solution)/shard_map/all_to_all | solution.py:248
  46.3 17.3 %collective-permute-start = (f32[6,22,8,128]{3,2,1,0:T(8,128)S(1)}, f32[6,22,8,128]{3,2,1,0:T(8,128)S(1)}, u32[]{:S(2)}, u32[]{:S(2)}) collective-permute-start(f32[6,22,8,128]{3,2,1,0:T(8,128)S(1)} %all-to-all-done.1.own.refs_0_), channel_id=1, source_target_pairs={{0,24},{24,48},{48,72},{72,96},{96,120},{120,144},{144,168},{168,1... | collective-permute-start | bytes 1622024 | tf_op jit(solution)/shard_map/ppermute | solution.py:233
  50.9 20.4 %collective-permute-start.1 = (f32[6,22,8,128]{3,2,1,0:T(8,128)S(1)}, f32[6,22,8,128]{3,2,1,0:T(8,128)S(1)}, u32[]{:S(2)}, u32[]{:S(2)}) collective-permute-start(f32[6,22,8,128]{3,2,1,0:T(8,128)S(1)} %all-to-all-done.1.own.refs_0_), channel_id=1, source_target_pairs={{24,0},{48,24},{72,48},{96,72},{120,96},{144,120},{168,144},{192,1... | collective-permute-start | bytes 1622024 | tf_op jit(solution)/shard_map/ppermute | solution.py:233
  55.6 18.7 %collective-permute-start.2 = (f32[6,22,8,128]{3,2,1,0:T(8,128)S(1)}, f32[6,22,8,128]{3,2,1,0:T(8,128)S(1)}, u32[]{:S(2)}, u32[]{:S(2)}) collective-permute-start(f32[6,22,8,128]{3,2,1,0:T(8,128)S(1)} %all-to-all-done.2.refs_3_), channel_id=1, source_target_pairs={{0,24},{24,48},{48,72},{72,96},{96,120},{120,144},{144,168},{168,1... | collective-permute-start | bytes 1622024 | tf_op jit(solution)/shard_map/ppermute | solution.py:233
  60.2 21.5 %collective-permute-start.3 = (f32[6,22,8,128]{3,2,1,0:T(8,128)S(1)}, f32[6,22,8,128]{3,2,1,0:T(8,128)S(1)}, u32[]{:S(2)}, u32[]{:S(2)}) collective-permute-start(f32[6,22,8,128]{3,2,1,0:T(8,128)S(1)} %all-to-all-done.2.refs_3_), channel_id=1, source_target_pairs={{24,0},{48,24},{72,48},{96,72},{120,96},{144,120},{168,144},{192,1... | collective-permute-start | bytes 1622024 | tf_op jit(solution)/shard_map/ppermute | solution.py:233
  71.7 10.6 %copy-start = (f32[22,32,384]{2,1,0:T(8,128)S(1)}, f32[22,32,384]{2,1,0:T(8,128)}, u32[]{:S(2)}) copy-start(f32[22,32,384]{2,1,0:T(8,128)} %variance.5) | copy-start | bytes 3244036
  83.8 52.0 %collective-permute-start.12 = (f32[11,32,256]{2,1,0:T(8,128)S(1)}, f32[11,32,256]{2,1,0:T(8,128)S(1)}, u32[]{:S(2)}, u32[]{:S(2)}) collective-permute-start(f32[11,32,256]{2,1,0:T(8,128)S(1)} %shard_map.46.refs_3_), channel_id=1, source_target_pairs={{0,24},{24,48},{48,72},{72,96},{96,120},{120,144},{144,168},{168,1... | collective-permute-start | bytes 1081352 | tf_op jit(solution)/shard_map/ppermute | solution.py:233
  85.7 39.1 %collective-permute-start.4 = (f32[22,16,128]{2,1,0:T(8,128)S(1)}, f32[22,16,128]{2,1,0:T(8,128)S(1)}, u32[]{:S(2)}, u32[]{:S(2)}) collective-permute-start(f32[22,16,128]{2,1,0:T(8,128)S(1)} %get-tuple-element.21), channel_id=1, source_target_pairs={{0,6},{6,12},{12,18},{18,0},{1,7},{7,13},{13,19},{19,1},{2,8},{8,1... | collective-permute-start | bytes 540680 | tf_op jit(solution)/shard_map/ppermute | solution.py:233
  98.4 29.5 %collective-permute-start.5 = (f32[22,16,128]{2,1,0:T(8,128)S(1)}, f32[22,16,128]{2,1,0:T(8,128)S(1)}, u32[]{:S(2)}, u32[]{:S(2)}) collective-permute-start(f32[22,16,128]{2,1,0:T(8,128)S(1)} %get-tuple-element.22), channel_id=1, source_target_pairs={{0,18},{6,0},{12,6},{18,12},{1,19},{7,1},{13,7},{19,13},{2,20},{8,... | collective-permute-start | bytes 540680 | tf_op jit(solution)/shard_map/ppermute | solution.py:233
  100.6 15.0 %collective-permute-start.6 = (f32[22,8,128]{2,1,0:T(8,128)S(1)}, f32[22,8,128]{2,1,0:T(8,128)S(1)}, u32[]{:S(2)}, u32[]{:S(2)}) collective-permute-start(f32[22,8,128]{2,1,0:T(8,128)S(1)} %get-tuple-element.23), channel_id=1, source_target_pairs={{0,6},{6,12},{12,18},{18,0},{1,7},{7,13},{13,19},{19,1},{2,8},{8,1... | collective-permute-start | bytes 270344 | tf_op jit(solution)/shard_map/ppermute | solution.py:233
  107.5 14.5 %collective-permute-start.7 = (f32[22,8,128]{2,1,0:T(8,128)S(1)}, f32[22,8,128]{2,1,0:T(8,128)S(1)}, u32[]{:S(2)}, u32[]{:S(2)}) collective-permute-start(f32[22,8,128]{2,1,0:T(8,128)S(1)} %get-tuple-element.24), channel_id=1, source_target_pairs={{0,18},{6,0},{12,6},{18,12},{1,19},{7,1},{13,7},{19,13},{2,20},{8,... | collective-permute-start | bytes 270344 | tf_op jit(solution)/shard_map/ppermute | solution.py:233
  115.6 22.1 %collective-permute-start.13 = (f32[11,32,256]{2,1,0:T(8,128)S(1)}, f32[11,32,256]{2,1,0:T(8,128)S(1)}, u32[]{:S(2)}, u32[]{:S(2)}) collective-permute-start(f32[11,32,256]{2,1,0:T(8,128)S(1)} %shard_map.46.refs_3_), channel_id=1, source_target_pairs={{24,0},{48,24},{72,48},{96,72},{120,96},{144,120},{168,144},{192,1... | collective-permute-start | bytes 1081352 | tf_op jit(solution)/shard_map/ppermute | solution.py:233
  122.1 15.7 %collective-permute-start.10 = (f32[11,32,256]{2,1,0:T(8,128)S(1)}, f32[11,32,256]{2,1,0:T(8,128)S(1)}, u32[]{:S(2)}, u32[]{:S(2)}) collective-permute-start(f32[11,32,256]{2,1,0:T(8,128)S(1)} %shard_map.45.refs_0_), channel_id=1, source_target_pairs={{0,24},{24,48},{48,72},{72,96},{96,120},{120,144},{144,168},{168,1... | collective-permute-start | bytes 1081352 | tf_op jit(solution)/shard_map/ppermute | solution.py:233
  124.8 15.0 %collective-permute-start.11 = (f32[11,32,256]{2,1,0:T(8,128)S(1)}, f32[11,32,256]{2,1,0:T(8,128)S(1)}, u32[]{:S(2)}, u32[]{:S(2)}) collective-permute-start(f32[11,32,256]{2,1,0:T(8,128)S(1)} %shard_map.45.refs_0_), channel_id=1, source_target_pairs={{24,0},{48,24},{72,48},{96,72},{120,96},{144,120},{168,144},{192,1... | collective-permute-start | bytes 1081352 | tf_op jit(solution)/shard_map/ppermute | solution.py:233
  129.7 13.1 %collective-permute-start.8 = (f32[22,32,128]{2,1,0:T(8,128)S(1)}, f32[22,32,128]{2,1,0:T(8,128)S(1)}, u32[]{:S(2)}, u32[]{:S(2)}) collective-permute-start(f32[22,32,128]{2,1,0:T(8,128)S(1)} %shard_map.44.own), channel_id=1, source_target_pairs={{0,24},{24,48},{48,72},{72,96},{96,120},{120,144},{144,168},{168,1... | collective-permute-start | bytes 1081352 | tf_op jit(solution)/shard_map/ppermute | solution.py:233
  135.8 14.4 %collective-permute-start.9 = (f32[22,32,128]{2,1,0:T(8,128)S(1)}, f32[22,32,128]{2,1,0:T(8,128)S(1)}, u32[]{:S(2)}, u32[]{:S(2)}) collective-permute-start(f32[22,32,128]{2,1,0:T(8,128)S(1)} %shard_map.44.own), channel_id=1, source_target_pairs={{24,0},{48,24},{72,48},{96,72},{120,96},{144,120},{168,144},{192,1... | collective-permute-start | bytes 1081352 | tf_op jit(solution)/shard_map/ppermute | solution.py:233
